TPU v7x, 32 devices: a whole 2x2x4 slice. The times are simulated.
32 devices in a mesh: group: 2 (over core), dp: 16 (over z, y, x).
Axes of the slice: x: 2, y: 2, z: 4, core: 2. Of those that a mesh axis runs over, the one named last changes fastest.
Arguments:
- patches: bfloat16 [2, 16, 512, 768], P(None, 'dp'), may hold values from -6 to 6
- segments: int32 [2, 16, 512], P(None, 'dp'), may hold values from 0 to 4, never falling along the last dimension, each value on 1 to 196 neighbouring positions
- positions: int32 [2, 16, 320], P(None, 'dp'), may hold values from 0 to 511, as said below
- owners: int32 [10752], replicated, may hold values from 0 to 10751, each once
- master: float32 [10752, 768], P(('group', 'dp')), may hold values from -0.21875 to 0.21875
- moment_one: float32 [10752, 768], P(('group', 'dp')), may hold values from -2.3841858e-06 to 2.3841858e-06
- moment_two: float32 [10752, 768], P(('group', 'dp')), may hold values from 3.8e-15 to 1.5e-14
- teacher: float32 [10752, 768], P(('group', 'dp')), may hold values from -0.21875 to 0.21875
- gains: float32 [4, 768], replicated, may hold values from 0.5 to 1.5
- gain_one: float32 [4, 768], replicated, may hold values from -2.2888184e-05 to 2.2888184e-05
- gain_two: float32 [4, 768], replicated, may hold values from 7.7e-13 to 3.1e-12
- teacher_gains: float32 [4, 768], replicated, may hold values from 0.5 to 1.5
- step_count: int32 [1], replicated, may hold values from 2 to 20
Outputs:
- loss_out: float32 [1], replicated
- clip_norm: float32 [1], replicated
- moment_one_new: float32 [10752, 768], P(('group', 'dp'))
- moment_two_new: float32 [10752, 768], P(('group', 'dp'))
- master_new: float32 [10752, 768], P(('group', 'dp'))
- teacher_new: float32 [10752, 768], P(('group', 'dp'))
- gain_one_new: float32 [4, 768], replicated
- gain_two_new: float32 [4, 768], replicated
Inputs may be any that keep to these rules, and one draw needn't show every extreme that they name: Within one row the 320 positions are distinct slots. `segments`: along a row segment ids never fall; id 4 is the padding at the row's end; each id covers 1 to 196 slots and some id covers exactly 196. owners is a permutation.
All inputs are finite; a program needn't handle non-finite values.
Results may differ from a plain program's by a relative error of at most 0.008.
The roundings to bfloat16 on the way count: a program that leaves them out, or rounds other values in their place, can miss the bound.
Values may be sent and summed in bfloat16 or wider, within the bound.
A program may use at most 320 MiB of HBM per device.

v0:
```python
import functools

import jax
import jax.numpy as jnp
from jax import lax
from jax.experimental import pallas as pl
from jax.experimental.pallas import tpu as pltpu
from jax.sharding import PartitionSpec as P

HEADS = 12
HEAD_DIM = 64
IMGS = 4
MASKED = 320
MICRO_BATCHES = 2
LANES = 128
SUBLANES = 8
TILE = SUBLANES * SUBLANES

SOFTMAX_TEMPER = 0.05
CLIP = 0.004
RATE = 0.05
BETA_ONE = 0.9
BETA_TWO = 0.999
ADAM_EPS = 1e-08
DECAY = 0.05
EMA_KEEP = 0.9
MASK_FILL = -1000000000.0

BF = jnp.bfloat16
F32 = jnp.float32
VMEM_LIMIT = 67_000_000
GELU_A = 0.7978845608028654
GELU_B = 0.044715


def nn(a, b):
    return jnp.dot(a, b, preferred_element_type=F32)


def nt(a, b):
    return lax.dot_general(a, b, (((1,), (1,)), ((), ())), preferred_element_type=F32)


def piece_rows(flat, width, inner):
    cuts = inner // width
    qkv, up = flat - 3 * width, flat - 6 * width
    inside = jnp.where(flat < 6 * width, (3 + qkv % 3) * width + qkv // 3, (6 + up % cuts) * width + up // cuts)
    return jnp.where((flat >= 3 * width) & (flat < 6 * width + inner), inside, flat)


def any_spec():
    return pl.BlockSpec(memory_space=pl.ANY)


def smem_spec():
    return pl.BlockSpec(memory_space=pltpu.SMEM)


MESH = pl.DeviceIdType.MESH
KERNEL_CHIPS = 16


def chip_grid(chips):
    sizes, turn, left, prime = [1, 1, 1], 0, chips, 2
    while left > 1:
        while left % prime:
            prime += 1
        sizes[turn % 3] *= prime
        turn += 1
        left //= prime
    return tuple(sizes)


def strides_of(grid):
    return (grid[1] * grid[2], grid[2], 1)


def coords_of(index, grid):
    return (index // (grid[1] * grid[2]), lax.rem(index // grid[2], grid[1]), lax.rem(index, grid[2]))


def guarded(conditions, action):
    conditions = [c for c in conditions if c is not None]
    if not conditions:
        return action()
    both = conditions[0]
    for c in conditions[1:]:
        both = jnp.logical_and(both, c)
    pl.when(both)(action)


def lanes_of(width):
    unit = width // 6
    orders = [((1, 0, 2), 2), ((2, 0, 1), 2), ((0, 2, 1), 1), ((0, 1, 2), 1)]
    routes, first = [], 0
    for order, share in orders:
        routes.append((order, first, share * unit))
        first += share * unit
    return routes


def offsets(length):
    if length <= 2:
        return list(range(length))
    return [0] + [sign * far for far in range(1, length) for sign in (1, -1)]


def route_events(grid, routes):
    events = []
    for c, (order, _, _) in enumerate(routes):
        stack = [()]
        for d in order:
            stack = [r + (o,) for r in stack for o in offsets(grid[d])]
        events += [(sum(abs(o) * 2**i for i, o in enumerate(r)), c, r) for r in stack]
    return [(c, r) for _, c, r in sorted(events, key=lambda e: e[0])]


def onward(grid, order, r):
    last = max([i for i in range(3) if r[i]], default=-1)
    outs = []
    if last >= 0 and grid[order[last]] > 2:
        outs.append((order[last], 1 if r[last] > 0 else -1))
    for d in order[last + 1 :]:
        if grid[d] == 2:
            outs.append((d, 1))
        elif grid[d] > 2:
            outs += [(d, 1), (d, -1)]
    return outs


def neighbour(me, coords, grid, d, sign):
    step = strides_of(grid)[d]
    if grid[d] == 2:
        return me + (1 - 2 * coords[d]) * step, None
    place = coords[d] + sign
    return me + sign * step, jnp.logical_and(place >= 0, place < grid[d])


def origin(me, coords, grid, order, r):
    index, conditions = me, []
    for d, o in zip(order, r):
        if o == 0:
            continue
        step = strides_of(grid)[d]
        if grid[d] == 2:
            index = index + (1 - 2 * coords[d]) * step
        else:
            place = coords[d] - o
            index = index - o * step
            conditions.append(jnp.logical_and(place >= 0, place < grid[d]))
    return index, conditions


def slot_of(grid, d, sign):
    first = sum([1 if n <= 2 else 2 for n in grid[:d]])
    return first if grid[d] <= 2 or sign > 0 else first + 1


def slots_of(grid):
    return sum([1 if n <= 2 else 2 for n in grid])


def greet(me, coords, grid, group):
    barrier = pltpu.get_barrier_semaphore()
    near = [neighbour(me, coords, grid, d, s) for d in range(3) for s in ((1,) if grid[d] == 2 else (1, -1)) if grid[d] > 1]
    for index, there in near:
        guarded([there], lambda: pl.semaphore_signal(barrier, 1, device_id={"dp": index}, device_id_type=MESH))
    pl.semaphore_signal(barrier, 1, device_id={"group": 1 - group}, device_id_type=MESH)
    pl.semaphore_wait(barrier, 1 + sum([1 if there is None else there.astype(jnp.int32) for _, there in near]))


def gather_kernel(grid, both, out, swap_sem, send_sem, recv_sem):
    group, me = lax.axis_index("group"), lax.axis_index("dp")
    coords = coords_of(me, grid)
    routes = lanes_of(both.shape[2])
    events = route_events(grid, routes)
    keep = pltpu.make_async_copy(both.at[group], out.at[me, group], swap_sem.at[2])
    keep.start()
    greet(me, coords, grid, group)
    swap = pltpu.make_async_remote_copy(
        both.at[1 - group], out.at[me, group], swap_sem.at[0], swap_sem.at[1], {"group": 1 - group}, MESH
    )
    swap.start()
    keep.wait()
    swap.wait()

    def visit(c, r, act):
        order, first, wide = routes[c]
        block, real = origin(me, coords, grid, order, r)
        part = out.at[block, :, :, first : first + wide]

        def run():
            copies = []
            for d, sign in onward(grid, order, r):
                index, there = neighbour(me, coords, grid, d, sign)
                copies.append(
                    (
                        there,
                        pltpu.make_async_remote_copy(
                            part,
                            part,
                            send_sem.at[c, slot_of(grid, d, sign), block],
                            recv_sem.at[c, block],
                            {"dp": index},
                            MESH,
                        ),
                    )
                )
            act(part, recv_sem.at[c, block], any(r), copies)

        guarded(real, run)

    def forward_on(part, arrival_sem, remote, copies):
        if remote:
            pltpu.make_async_remote_copy(part, part, swap_sem.at[0], arrival_sem, {"dp": me}, MESH).wait_recv()
        for there, copy in copies:
            guarded([there], copy.start)

    def finish(part, arrival_sem, remote, copies):
        for there, copy in copies:
            guarded([there], copy.wait_send)

    for c, r in events:
        visit(c, r, forward_on)
    for c, r in events:
        visit(c, r, finish)


def gather_weights(both, chips):
    grid = chip_grid(chips)
    _, rows, width = both.shape
    return pl.pallas_call(
        functools.partial(gather_kernel, grid),
        name="gather_weights",
        out_shape=jax.ShapeDtypeStruct((chips, 2, rows, width), BF),
        in_specs=[pl.BlockSpec(memory_space=pltpu.VMEM)],
        out_specs=any_spec(),
        scratch_shapes=[
            pltpu.SemaphoreType.DMA((3,)),
            pltpu.SemaphoreType.DMA((4, slots_of(grid), chips)),
            pltpu.SemaphoreType.DMA((4, chips)),
        ],
        compiler_params=pltpu.CompilerParams(
            collective_id=1, has_side_effects=True, vmem_limit_bytes=VMEM_LIMIT
        ),
    )(both)


def reduce_kernel(grid, blocked, out, acc, heard, load_sem, half_sem, send_sem, recv_sem):
    group, me = lax.axis_index("group"), lax.axis_index("dp")
    coords = coords_of(me, grid)
    rows, width = out.shape
    routes = lanes_of(width)
    events = route_events(grid, routes)[::-1]
    across = slots_of(grid)
    tall = max([t for t in range(16, 49, 16) if rows % t == 0], default=rows)

    def spot(c, r):
        return tuple(r[routes[c][0].index(d)] for d in range(3))

    firsts = list(dict.fromkeys([spot(c, r) for c, r in events]))
    greet(me, coords, grid, group)

    def load(where, act):
        block, real = origin(me, coords, grid, (0, 1, 2), where)
        local = pltpu.make_async_copy(blocked.at[group, block], acc.at[block], load_sem.at[block])
        half = pltpu.make_async_remote_copy(
            blocked.at[1 - group, block],
            heard.at[across, block],
            half_sem.at[0, block],
            half_sem.at[1, block],
            {"group": 1 - group},
            MESH,
        )
        guarded(real, lambda: act(local, half))

    def load_start(local, half):
        half.start()
        local.start()

    def load_wait(local, half):
        local.wait()
        half.wait_recv()

    def load_end(local, half):
        half.wait_send()

    for where in firsts:
        load(where, load_start)

    def parent(c, r, block):
        order, first, wide = routes[c]
        i = max([i for i in range(3) if r[i]])
        sign = 1 if r[i] > 0 else -1
        index, _ = neighbour(me, coords, grid, order[i], -sign)
        slot = slot_of(grid, order[i], sign)
        return pltpu.make_async_remote_copy(
            acc.at[block, :, first : first + wide],
            heard.at[slot, block, :, first : first + wide],
            send_sem.at[c, block],
            recv_sem.at[c, slot, block],
            {"dp": index},
            MESH,
        )

    def visit(c, r):
        order, first, wide = routes[c]
        block, real = origin(me, coords, grid, order, r)

        def run():
            children = [(slot_of(grid, d, s), neighbour(me, coords, grid, d, s)[1]) for d, s in onward(grid, order, r)]
            for slot, there in children:
                part = heard.at[slot, block, :, first : first + wide]
                arrival = pltpu.make_async_remote_copy(
                    part, part, send_sem.at[c, block], recv_sem.at[c, slot, block], {"dp": me}, MESH
                )
                guarded([there], arrival.wait_recv)
            children = [(across, None)] + children

            if any(r):
                for slot, there in children:

                    def total(slot=slot):
                        def piece(k, carry):
                            at = (pl.ds(pl.multiple_of(k * tall, tall), tall), slice(first, first + wide))
                            acc[(block,) + at] = (
                                acc[(block,) + at].astype(F32) + heard[(slot, block) + at].astype(F32)
                            ).astype(BF)
                            return carry

                        lax.fori_loop(0, rows // tall, piece, 0)

                    guarded([there], total)
                parent(c, r, block).start()
            else:

                def first_piece(k, carry):
                    at = (pl.ds(pl.multiple_of(k * tall, tall), tall), slice(first, first + wide))
                    out[at] = acc[(block,) + at].astype(F32)
                    return carry

                lax.fori_loop(0, rows // tall, first_piece, 0)
                for slot, there in children:

                    def total(slot=slot):
                        def piece(k, carry):
                            at = (pl.ds(pl.multiple_of(k * tall, tall), tall), slice(first, first + wide))
                            out[at] = out[at] + heard[(slot, block) + at].astype(F32)
                            return carry

                        lax.fori_loop(0, rows // tall, piece, 0)

                    guarded([there], total)

        guarded(real, run)

    ready = set()
    for c, r in events:
        if spot(c, r) not in ready:
            ready.add(spot(c, r))
            load(spot(c, r), load_wait)
        visit(c, r)
    for c, r in events:
        if any(r):
            block, real = origin(me, coords, grid, routes[c][0], r)
            guarded(real, parent(c, r, block).wait_send)
    for where in firsts:
        load(where, load_end)


def reduce_grads(blocked, chips):
    grid = chip_grid(chips)
    _, _, rows, width = blocked.shape
    return pl.pallas_call(
        functools.partial(reduce_kernel, grid),
        name="reduce_grads",
        out_shape=jax.ShapeDtypeStruct((rows, width), F32),
        in_specs=[any_spec()],
        out_specs=pl.BlockSpec(memory_space=pltpu.VMEM),
        scratch_shapes=[
            pltpu.VMEM((chips, rows, width), BF),
            pltpu.VMEM((slots_of(grid) + 1, chips, rows, width), BF),
            pltpu.SemaphoreType.DMA((chips,)),
            pltpu.SemaphoreType.DMA((2, chips)),
            pltpu.SemaphoreType.DMA((4, chips)),
            pltpu.SemaphoreType.DMA((4, slots_of(grid), chips)),
        ],
        compiler_params=pltpu.CompilerParams(
            collective_id=2, has_side_effects=True, vmem_limit_bytes=VMEM_LIMIT
        ),
    )(blocked)


def exchange_kernel(*refs):
    count = (len(refs) - 7) // 2
    bank, states, banks = refs[count], refs[count + 1 : 2 * count + 1], refs[2 * count + 1]
    state_send, state_recv, send_sem, recv_sem, own_sem = refs[2 * count + 2 :]
    group, me = lax.axis_index("group"), lax.axis_index("dp")
    chips = banks.shape[0]
    barrier = pltpu.get_barrier_semaphore()

    def hail(target):
        def one(k, carry):
            pl.semaphore_signal(barrier, 1, device_id=(target, lax.rem(me + k, chips)), device_id_type=MESH)
            return carry

        return one

    @pl.when(group == 0)
    def _():
        lax.fori_loop(1, chips, hail(0), 0)
        lax.fori_loop(0, chips, hail(1), 0)

    @pl.when(group == 1)
    def _():
        lax.fori_loop(0, chips, hail(0), 0)

    pl.semaphore_wait(barrier, chips + (1 - group) * (chips - 1))

    def crossing(k):
        ref = states[k]
        if k == count - 1:
            part = ref.at[1]
        elif len(ref.shape) == 3 and ref.shape[0] == 3:
            part = ref.at[:, : ref.shape[1] // MICRO_BATCHES, :]
        else:
            part = ref.at[0]
        return pltpu.make_async_remote_copy(
            part, part, state_send.at[k], state_recv.at[k], {"group": 1 - group}, MESH
        )

    def note(core, k):
        return pltpu.make_async_remote_copy(
            bank.at[core],
            banks.at[me],
            send_sem.at[core, k],
            recv_sem.at[me],
            (core, lax.rem(me + k, chips)),
            MESH,
        )

    def each(core, act):
        def one(k, carry):
            act(note(core, k))
            return carry

        return one

    def take(k, carry):
        pltpu.make_async_remote_copy(
            bank.at[0], banks.at[k], send_sem.at[0, 0], recv_sem.at[k], (1 - group, me), MESH
        ).wait_recv()
        return carry

    @pl.when(group == 0)
    def _():
        own = pltpu.make_async_copy(bank.at[0], banks.at[me], own_sem)
        own.start()
        lax.fori_loop(1, chips, each(0, lambda copy: copy.start()), 0)
        lax.fori_loop(0, chips, each(1, lambda copy: copy.start()), 0)
        targets = crossing(count - 1)
        targets.start()
        own.wait()
        lax.fori_loop(1, chips, lambda k, carry: take(lax.rem(me + k, chips), carry), 0)
        for k in range(count - 1):
            crossing(k).wait_recv()
        lax.fori_loop(1, chips, each(0, lambda copy: copy.wait_send()), 0)
        lax.fori_loop(0, chips, each(1, lambda copy: copy.wait_send()), 0)
        targets.wait_send()

    @pl.when(group == 1)
    def _():
        copies = [crossing(k) for k in range(count - 1)]
        for copy in copies:
            copy.start()
        lax.fori_loop(0, chips, take, 0)
        crossing(count - 1).wait_recv()
        for copy in copies:
            copy.wait_send()


def exchange_states(states, bank, chips):
    count = len(states)
    outs = pl.pallas_call(
        exchange_kernel,
        name="exchange_states",
        out_shape=tuple(jax.ShapeDtypeStruct(a.shape, a.dtype) for a in states)
        + (jax.ShapeDtypeStruct((chips,) + bank.shape[1:], BF),),
        in_specs=[any_spec()] * (count + 1),
        out_specs=(any_spec(),) * (count + 1),
        scratch_shapes=[
            pltpu.SemaphoreType.DMA((count,)),
            pltpu.SemaphoreType.DMA((count,)),
            pltpu.SemaphoreType.DMA((2, chips)),
            pltpu.SemaphoreType.DMA((chips,)),
            pltpu.SemaphoreType.DMA,
        ],
        input_output_aliases={k: k for k in range(count)},
        compiler_params=pltpu.CompilerParams(collective_id=3, has_side_effects=True),
    )(*states, bank)
    return outs[:-1], outs[-1]


def sum_kernel(grid, tile, out, heard, send_sem, recv_sem):
    group, me = lax.axis_index("group"), lax.axis_index("dp")
    coords = coords_of(me, grid)
    lengths = (2,) + grid
    mine = (group,) + coords
    peers = []
    for s, length in enumerate(lengths):
        for k in range(1, length):
            other = lax.rem(mine[s] + k, length)
            if s == 0:
                peers.append((s, k, (other, me)))
            else:
                peers.append((s, k, (group, me + (other - mine[s]) * strides_of(grid)[s - 1])))
    barrier = pltpu.get_barrier_semaphore()
    for _, _, device in peers:
        pl.semaphore_signal(barrier, 1, device_id=device, device_id_type=MESH)
    pl.semaphore_wait(barrier, len(peers))
    out[...] = tile[...]
    for s, length in enumerate(lengths):
        if length == 1:
            continue
        heard[s, mine[s]] = out[...]
        copies = [
            pltpu.make_async_remote_copy(
                heard.at[s, mine[s]], heard.at[s, mine[s]], send_sem.at[s, k], recv_sem.at[s, mine[s]], device, MESH
            )
            for t, k, device in peers
            if t == s
        ]
        for copy in copies:
            copy.start()
        for k in range(1, length):
            other = lax.rem(mine[s] + k, length)
            pltpu.make_async_remote_copy(
                heard.at[s, other], heard.at[s, other], send_sem.at[s, k], recv_sem.at[s, other], (group, me), MESH
            ).wait_recv()
        total = heard[s, 0]
        for k in range(1, length):
            total = total + heard[s, k]
        out[...] = total
        for copy in copies:
            copy.wait_send()


def sum_tiles(tile, chips):
    grid = chip_grid(chips)
    most = max((2,) + grid)
    return pl.pallas_call(
        functools.partial(sum_kernel, grid),
        name="sum_tiles",
        out_shape=jax.ShapeDtypeStruct(tile.shape, F32),
        in_specs=[pl.BlockSpec(memory_space=pltpu.VMEM)],
        out_specs=pl.BlockSpec(memory_space=pltpu.VMEM),
        scratch_shapes=[
            pltpu.VMEM((4, most) + tile.shape, F32),
            pltpu.SemaphoreType.DMA((4, most)),
            pltpu.SemaphoreType.DMA((4, most)),
        ],
        compiler_params=pltpu.CompilerParams(collective_id=4, has_side_effects=True),
    )(tile)


def place_kernel(spots, model, out, rows_scr, inbuf, stage, outbuf, in_sem, out_sem):
    chips, cores, rows, width = model.shape
    blocks = cores * chips
    cols = width // LANES
    deep, wide = inbuf.shape[0], outbuf.shape[0]
    group = max([g for g in range(1, 17) if rows % g == 0])

    def fetch(b, slot):
        return pltpu.make_async_copy(model.at[lax.rem(b, chips), b // chips], inbuf.at[slot], in_sem.at[slot])

    for b in range(deep - 1):
        fetch(b, b).start()

    def block(b, carry):
        slot = lax.rem(b, deep)
        fetch(b, slot).wait()

        @pl.when(b + deep - 1 < blocks)
        def _():
            fetch(b + deep - 1, lax.rem(b + deep - 1, deep)).start()

        for c in range(cols):
            stage[pl.ds(c, rows, stride=SUBLANES), :] = inbuf[slot, :, c * LANES : (c + 1) * LANES].astype(F32)

        def move(q, carry):
            first = q * group
            to = [spots[b * rows + first + j] for j in range(group)]
            held = [stage[pl.ds(pl.multiple_of((first + j) * SUBLANES, SUBLANES), SUBLANES), :] for j in range(group)]
            for j in range(group):
                rows_scr[pl.ds(to[j], SUBLANES, stride=SUBLANES), :] = held[j]
            return carry

        return lax.fori_loop(0, rows // group, move, carry)

    lax.fori_loop(0, blocks, block, 0)
    pieces = out.shape[0]
    for u in range(pieces):
        slot = u % wide
        if u >= wide:
            pltpu.make_async_copy(outbuf.at[slot], out.at[u - wide], out_sem.at[slot]).wait()

        def pack(k, carry):
            to = pl.ds(pl.multiple_of(k * 16, 16), 16)
            for c in range(cols):
                first = (u * width // SUBLANES + 2 * k) * TILE + c * SUBLANES
                halves = [rows_scr[pl.ds(pl.multiple_of(first + TILE * h, SUBLANES), SUBLANES), :] for h in range(2)]
                outbuf[slot, to, c * LANES : (c + 1) * LANES] = jnp.concatenate(halves, axis=0).astype(BF)
            return carry

        lax.fori_loop(0, width // 16, pack, 0)
        pltpu.make_async_copy(outbuf.at[slot], out.at[u], out_sem.at[slot]).start()
    for u in range(pieces - wide, pieces):
        pltpu.make_async_copy(outbuf.at[u % wide], out.at[u], out_sem.at[u % wide]).wait()


def place_weights(spots, model):
    _, _, rows, width = model.shape
    total = spots.shape[0]
    return pl.pallas_call(
        place_kernel,
        name="place_weights",
        out_shape=jax.ShapeDtypeStruct((total // width, width, width), BF),
        in_specs=[smem_spec(), any_spec()],
        out_specs=any_spec(),
        scratch_shapes=[
            pltpu.VMEM((total * SUBLANES, LANES), F32),
            pltpu.VMEM((8, rows, width), BF),
            pltpu.VMEM((rows * SUBLANES, LANES), F32),
            pltpu.VMEM((4, width, width), BF),
            pltpu.SemaphoreType.DMA((8,)),
            pltpu.SemaphoreType.DMA((4,)),
        ],
        compiler_params=pltpu.CompilerParams(vmem_limit_bytes=VMEM_LIMIT),
    )(spots, model)


def layer_stats(tensor):
    centre = tensor - jnp.mean(tensor, axis=-1, keepdims=True)
    scaled = lax.rsqrt(jnp.mean(centre * centre, axis=-1, keepdims=True) + 1e-06)
    return centre * scaled, scaled


def column_of(row):
    n = row.shape[1]
    eye = lax.broadcasted_iota(jnp.int32, (n, n), 0) == lax.broadcasted_iota(jnp.int32, (n, n), 1)
    return jnp.sum(jnp.where(eye, row, 0), axis=1, keepdims=True)


def flag_column(pos, slots):
    hit = lax.broadcasted_iota(jnp.int32, (slots, pos.shape[1]), 0) == pos
    return jnp.max(jnp.where(hit, 1, 0), axis=1, keepdims=True)


def fill_bias(bias, seg_col, seg_row):
    bias[...] = jnp.where(seg_col == seg_row, 0.0, MASK_FILL)


def half(x, h):
    low = lax.broadcasted_iota(jnp.int32, (1, LANES), 1) < HEAD_DIM
    keep = low if h == 0 else jnp.logical_not(low)
    return jnp.where(keep, x, jnp.zeros_like(x))


def fwd_kernel(role, patch, seg, pos, gain, w_hbm, e_out, qkv, lse, o_out, x1_out, x2_out, tgt, bank, w, bias, sem):
    i = pl.program_id(0)
    slots, width = patch.shape[1:]
    pieces = w_hbm.shape[0]
    cuts = (pieces - 6) // 2
    order = [0, 3, 4, 5, 1]
    for j in range(cuts):
        order += [6 + j, 6 + cuts + j]

    @pl.when(i == 0)
    def _():
        for u in order:
            pltpu.make_async_copy(w_hbm.at[u], w.at[u], sem.at[u]).start()

    def need(u):
        @pl.when(i == 0)
        def _():
            pltpu.make_async_copy(w_hbm.at[u], w.at[u], sem.at[u]).wait()

    seg_row = seg[0]
    seg_col = column_of(seg_row)
    fill_bias(bias, seg_col, seg_row)
    flags = flag_column(pos[0], slots) * role[0]
    need(0)
    e = nn(patch[0], w[0])
    e = jnp.where(flags > 0, gain[3:4, :], e)
    e_out[0] = e
    a = (layer_stats(e)[0] * gain[0:1, :]).astype(BF)
    for j in range(3):
        need(3 + j)
        qkv[j] = nn(a, w[3 + j]).astype(BF)

    def pair(p, carry):
        cs = pl.ds(pl.multiple_of(p * LANES, LANES), LANES)
        q2, k2, v2 = qkv[0, :, cs], qkv[1, :, cs], qkv[2, :, cs]
        k2 = k2 * jnp.asarray(HEAD_DIM**-0.5, BF)
        v_t = v2.T
        outs = []
        for h in range(2):
            s = nt(half(k2, h), q2) + bias[...]
            top = jnp.max(s, axis=0, keepdims=True)
            ex = jnp.exp(s - top)
            total = jnp.sum(ex, axis=0, keepdims=True)
            lse[0, pl.ds(2 * p + h, 1), :] = top + jnp.log(total)
            probs = (ex * (1.0 / total)).astype(BF)
            outs.append(nn(v_t[h * HEAD_DIM : (h + 1) * HEAD_DIM, :], probs))
        o_out[0, :, cs] = jnp.concatenate(outs, axis=0).T.astype(BF)
        return carry

    lax.fori_loop(0, HEADS // 2, pair, 0)
    need(1)
    x1 = e_out[0] + nn(o_out[0], w[1])
    x1_out[0] = x1
    a2 = (layer_stats(x1)[0] * gain[1:2, :]).astype(BF)
    acc = x1
    for j in range(cuts):
        need(6 + j)
        hid = nn(a2, w[6 + j])
        act = (hid * (0.5 * (1.0 + jnp.tanh(GELU_A * (hid + GELU_B * hid * hid * hid))))).astype(BF)
        need(6 + cuts + j)
        acc = acc + nn(act, w[6 + cuts + j])
    x2_out[0] = acc

    @pl.when(role[0] == 0)
    def _():
        t = layer_stats(x2_out[0])[0].astype(BF)
        tgt[0] = t
        t = t.astype(F32)
        for m in range(IMGS):
            inside = seg_col == m
            size = jnp.sum(jnp.where(inside, 1.0, 0.0), axis=0, keepdims=True)
            pooled = jnp.sum(jnp.where(inside, t, 0.0), axis=0, keepdims=True) / size
            unit = pooled * lax.rsqrt(jnp.sum(pooled * pooled, axis=-1, keepdims=True) + 1e-06)
            bank[0, m : m + 1, :] = unit.astype(BF)


def forward(role, patch, seg, pos, gain, w):
    batches, slots, width = patch.shape
    pieces = w.shape[0]
    tok = lambda dt: jax.ShapeDtypeStruct((batches, slots, width), dt)
    row = pl.BlockSpec((1, slots, width), lambda i: (i, 0, 0))
    return pl.pallas_call(
        fwd_kernel,
        name="forward",
        grid=(batches,),
        out_shape=(
            tok(F32),
            jax.ShapeDtypeStruct((3, batches * slots, width), BF),
            jax.ShapeDtypeStruct((batches, HEADS, slots), F32),
            tok(BF),
            tok(F32),
            tok(F32),
            tok(BF),
            jax.ShapeDtypeStruct((batches, IMGS, width), BF),
        ),
        in_specs=[
            smem_spec(),
            row,
            pl.BlockSpec((1, 1, slots), lambda i: (i, 0, 0)),
            pl.BlockSpec((1, 1, pos.shape[2]), lambda i: (i, 0, 0)),
            pl.BlockSpec((4, width), lambda i: (0, 0)),
            any_spec(),
        ],
        out_specs=(
            row,
            pl.BlockSpec((3, slots, width), lambda i: (0, i, 0)),
            pl.BlockSpec((1, HEADS, slots), lambda i: (i, 0, 0)),
            row,
            row,
            row,
            row,
            pl.BlockSpec((1, IMGS, width), lambda i: (i, 0, 0)),
        ),
        scratch_shapes=[
            pltpu.VMEM((pieces, width, width), BF),
            pltpu.VMEM((slots, slots), F32),
            pltpu.SemaphoreType.DMA((pieces,)),
        ],
        compiler_params=pltpu.CompilerParams(vmem_limit_bytes=VMEM_LIMIT),
        cost_estimate=pl.CostEstimate(
            flops=2 * batches * slots * width * width * pieces, bytes_accessed=2 * w.size, transcendentals=0
        ),
    )(role, patch, seg, pos, gain, w)


def norm_back(grad_out, normed, scaled, gain_vec):
    grad_hat = grad_out * gain_vec
    inner = jnp.mean(grad_hat * normed, axis=-1, keepdims=True)
    grad_in = scaled * (grad_hat - jnp.mean(grad_hat, axis=-1, keepdims=True) - normed * inner)
    return grad_in, jnp.sum(grad_out * normed, axis=0, keepdims=True)


def bwd_kernel(
    listed, place, seg, pos, gain, lse, banks, e_hbm, qkv_hbm, x1_hbm, x2_hbm, tgt_hbm, w_own, w_far,
    head_out, attn_out, ffn_out, act_out, de_out, mid_out, pred_out, dqkv_out, du_out, down_out, small,
    w, bias, top_scr, pool_scr, e_in, qkv, x1_in, x2_in, tgt,
    head_v, attn_v, ffn_v, act_v, de_v, mid_v, pred_v, dqkv, du_v, down_v, sem, in_sem, out_sem,
):
    role = place[0]
    slots, width = e_in.shape
    pieces = w_own.shape[0]
    cuts = (pieces - 6) // 2
    tokens = pl.ds(pl.multiple_of(role * slots, slots), slots)

    def bring(k, source, target):
        copy = pltpu.make_async_copy(source, target, in_sem.at[k])
        copy.start()
        return copy

    def bring_piece(u):
        @pl.when(role == 0)
        def _():
            pltpu.make_async_copy(w_far.at[u], w.at[u - 1], sem.at[u]).start()

        @pl.when(role != 0)
        def _():
            pltpu.make_async_copy(w_own.at[u], w.at[u - 1], sem.at[u]).start()

    def need(u):
        pltpu.make_async_copy(w_own.at[u], w.at[u - 1], sem.at[u]).wait()

    taken = []

    def keep(source, target):
        copy = pltpu.make_async_copy(source, target, out_sem.at[len(taken)])
        copy.start()
        taken.append(copy)

    x2_copy = bring(0, x2_hbm.at[role], x2_in)
    bring_piece(2)
    tgt_copy = bring(1, tgt_hbm.at[role], tgt)
    x1_copy = bring(2, x1_hbm.at[role], x1_in)
    for j in range(cuts):
        bring_piece(6 + cuts + j)
        bring_piece(6 + j)
    bring_piece(1)
    qkv_copy = bring(3, qkv_hbm.at[:, tokens, :], qkv)
    for j in range(3):
        bring_piece(3 + j)
    e_copy = bring(4, e_hbm.at[role], e_in)
    small[...] = jnp.zeros_like(small)

    seg_row = seg[role]
    seg_col = column_of(seg_row)
    fill_bias(bias, seg_col, seg_row)
    flags = flag_column(pos[role], slots)
    x2_copy.wait()
    n3, r3 = layer_stats(x2_in[...])
    head_in = (n3 * gain[2:3, :]).astype(BF)
    head_v[...] = head_in
    keep(head_v, head_out.at[0])
    need(2)
    pred = nn(head_in, w[1])
    valid = jnp.where(seg_col < IMGS, flags, 0).astype(F32)
    tgt_copy.wait()
    diff = pred - tgt[...].astype(F32)
    size = jnp.abs(diff)
    huber = jnp.where(size < 1.0, 0.5 * diff * diff, size - 0.5)
    regress = jnp.sum(jnp.sum(valid * huber, axis=1, keepdims=True), axis=0, keepdims=True)
    count = listed[0] * width
    grad_pred = valid * (jnp.clip(diff, -1.0, 1.0) / count)
    pool_scr[...] = jnp.zeros_like(pool_scr)
    for m in range(IMGS):
        inside = seg_col == m
        tally = jnp.sum(jnp.where(inside, 1.0, 0.0), axis=0, keepdims=True)
        pool_scr[m : m + 1, :] = jnp.sum(jnp.where(inside, pred, 0.0), axis=0, keepdims=True) / tally
    pooled = pool_scr[...]
    length = lax.rsqrt(jnp.sum(pooled * pooled, axis=-1, keepdims=True) + 1e-06)
    unit = pooled * length
    memory = banks[...]
    choices = memory.shape[0]
    logits = nt(unit.astype(BF), memory) / SOFTMAX_TEMPER
    row_id = lax.broadcasted_iota(jnp.int32, logits.shape, 0)
    real = row_id < IMGS
    picked = jnp.where(
        real & (lax.broadcasted_iota(jnp.int32, logits.shape, 1) == place[1] * IMGS + row_id), 1.0, 0.0
    )
    peak = jnp.max(logits, axis=-1, keepdims=True)
    ex = jnp.exp(logits - peak)
    total = jnp.sum(ex, axis=-1, keepdims=True)
    each = peak + jnp.log(total) - jnp.sum(logits * picked, axis=-1, keepdims=True)
    contrast = jnp.sum(jnp.where(real[:, 0:1], each, 0.0), axis=0, keepdims=True)
    scale = choices * MICRO_BATCHES
    grad_logits = (jnp.where(real, ex / total - picked, 0.0) / scale / SOFTMAX_TEMPER).astype(BF)
    grad_unit = nn(grad_logits, memory)
    grad_pool = length * (grad_unit - unit * jnp.sum(grad_unit * unit, axis=1, keepdims=True))
    pool_scr[...] = grad_pool
    for m in range(IMGS):
        inside = seg_col == m
        tally = jnp.sum(jnp.where(inside, 1.0, 0.0), axis=0, keepdims=True)
        grad_pred = grad_pred + jnp.where(inside, pool_scr[m : m + 1, :] / tally, 0.0)
    low = grad_pred.astype(BF)
    pred_v[...] = low
    keep(pred_v, pred_out.at[0])
    loss = regress / count + contrast / scale
    small[4:5, :] += jnp.broadcast_to(loss, (1, width))
    grad_top, gain_three = norm_back(nt(low, w[1]), n3, r3, gain[2:3, :])
    small[2:3, :] += gain_three
    top_scr[...] = grad_top
    down = grad_top.astype(BF)
    down_v[...] = down
    keep(down_v, down_out.at[0])
    x1_copy.wait()
    n2, r2 = layer_stats(x1_in[...])
    ffn_in = (n2 * gain[1:2, :]).astype(BF)
    ffn_v[...] = ffn_in
    keep(ffn_v, ffn_out.at[0])
    acc = None
    for j in range(cuts):
        need(6 + cuts + j)
        grad_act = nt(down, w[5 + cuts + j])
        need(6 + j)
        hid = nn(ffn_in, w[5 + j])
        th = jnp.tanh(GELU_A * (hid + GELU_B * hid * hid * hid))
        cdf = 0.5 * (1.0 + th)
        act_v[j] = (hid * cdf).astype(BF)
        keep(act_v.at[j], act_out.at[j])
        slope = cdf + hid * (0.5 * (1.0 - th * th)) * (GELU_A * (1.0 + 3.0 * GELU_B * hid * hid))
        du = (grad_act * slope).astype(BF)
        du_v[j] = du
        keep(du_v.at[j], du_out.at[j])
        part = nt(du, w[5 + j])
        acc = part if acc is None else acc + part
    grad_ffn, gain_two = norm_back(acc, n2, r2, gain[1:2, :])
    small[1:2, :] += gain_two
    mid = top_scr[...] + grad_ffn
    top_scr[...] = mid
    mid_low = mid.astype(BF)
    mid_v[...] = mid_low
    keep(mid_v, mid_out.at[0])
    need(1)
    de_v[...] = nt(mid_low, w[0]).astype(BF)
    qkv_copy.wait()

    def pair(p, carry):
        cs = pl.ds(pl.multiple_of(p * LANES, LANES), LANES)
        q2, k2, v2, g2 = qkv[0, :, cs], qkv[1, :, cs], qkv[2, :, cs], de_v[:, cs]
        k_scaled = k2 * jnp.asarray(HEAD_DIM**-0.5, BF)
        k_t = k2.T
        dq, dk, dv = [], 0.0, 0.0
        for h in range(2):
            s = nt(half(k_scaled, h), q2) + bias[...]
            probs = jnp.exp(s - lse[role, pl.ds(2 * p + h, 1), :])
            dp = nt(half(v2, h), g2)
            centre = jnp.sum(probs * dp, axis=0, keepdims=True)
            ds = (probs * (dp - centre)).astype(BF)
            dv = dv + nn(probs.astype(BF), half(g2, h))
            dk = dk + nn(ds, half(q2, h))
            dq.append(nn(k_t[h * HEAD_DIM : (h + 1) * HEAD_DIM, :], ds))
        dqkv[0, :, cs] = (jnp.concatenate(dq, axis=0) * HEAD_DIM**-0.5).T.astype(BF)
        dqkv[1, :, cs] = (dk * HEAD_DIM**-0.5).astype(BF)
        dqkv[2, :, cs] = dv.astype(BF)
        return carry

    lax.fori_loop(0, HEADS // 2, pair, 0)
    keep(dqkv, dqkv_out)
    acc = None
    for j in range(3):
        need(3 + j)
        part = nt(dqkv[j], w[2 + j])
        acc = part if acc is None else acc + part
    e_copy.wait()
    n1, r1 = layer_stats(e_in[...])
    attn_v[...] = (n1 * gain[0:1, :]).astype(BF)
    keep(attn_v, attn_out.at[0])
    grad_attn, gain_one = norm_back(acc, n1, r1, gain[0:1, :])
    small[0:1, :] += gain_one
    start = top_scr[...] + grad_attn
    hidden_slot = flags > 0
    small[3:4, :] += jnp.sum(jnp.where(hidden_slot, start, 0.0), axis=0, keepdims=True)
    de_v[...] = jnp.where(hidden_slot, 0.0, start).astype(BF)
    keep(de_v, de_out.at[0])
    for copy in taken:
        copy.wait()


def backward(listed, place, seg, pos, gain, lse, banks, e, qkv, x1, x2, tgt, w_own, w_far):
    _, slots, width = e.shape
    pieces = w_own.shape[0]
    cuts = (pieces - 6) // 2
    counts = (1, 1, 1, cuts, 1, 1, 1, 3, cuts, 1)
    vmem = pl.BlockSpec(memory_space=pltpu.VMEM)
    tok = lambda n, dt: pltpu.VMEM((n, slots, width) if n > 1 else (slots, width), dt)
    return pl.pallas_call(
        bwd_kernel,
        name="backward",
        out_shape=tuple(jax.ShapeDtypeStruct((n, slots, width), BF) for n in counts)
        + (jax.ShapeDtypeStruct((SUBLANES, width), F32),),
        in_specs=[smem_spec(), smem_spec()] + [vmem] * 5 + [any_spec()] * 7,
        out_specs=(any_spec(),) * len(counts) + (vmem,),
        scratch_shapes=[
            pltpu.VMEM((pieces - 1, width, width), BF),
            pltpu.VMEM((slots, slots), F32),
            pltpu.VMEM((slots, width), F32),
            pltpu.VMEM((SUBLANES, width), F32),
            tok(1, F32),
            tok(3, BF),
            tok(1, F32),
            tok(1, F32),
            tok(1, BF),
        ]
        + [tok(n, BF) for n in counts]
        + [
            pltpu.SemaphoreType.DMA((pieces,)),
            pltpu.SemaphoreType.DMA((5,)),
            pltpu.SemaphoreType.DMA((sum(counts),)),
        ],
        compiler_params=pltpu.CompilerParams(vmem_limit_bytes=VMEM_LIMIT),
    )(listed, place, seg, pos, gain, lse, banks, e, qkv, x1, x2, tgt, w_own, w_far)


def grads_kernel(
    plan, role, places, patch, mixed, head, attn, ffn, act, de, mid, pred, dqkv, du, down, out,
    rows_scr, x_buf, x_t, g_buf, stage, outbuf, x_sem, g_sem, out_sem,
):
    blocks, rows, width = out.shape
    cols = width // LANES
    deep, wide_out = x_buf.shape[0], outbuf.shape[0]
    group = max([g for g in range(SUBLANES, 49, SUBLANES) if rows % g == 0], default=rows)
    lefts = {"patch": patch, "mixed": mixed, "head": head, "attn": attn, "ffn": ffn, "act": act}
    rights = {"de": de, "mid": mid, "pred": pred, "dqkv": dqkv, "du": du, "down": down}

    def left_of(key):
        name, index = key
        return lefts[name].at[role[0] if name in ("patch", "mixed") else index]

    lcopies, rcopies = [], []
    lkeys, rkeys = [], []
    steps = []
    for u, (left, right) in enumerate(plan):
        if not lkeys or lkeys[-1] != left:
            slot = len(lkeys) % deep
            lcopies.append(pltpu.make_async_copy(left_of(left), x_buf.at[slot], x_sem.at[slot]))
            lkeys.append(left)
            fresh_l = True
        else:
            fresh_l = False
        if not rkeys or rkeys[-1] != right:
            slot = len(rkeys) % deep
            rcopies.append(pltpu.make_async_copy(rights[right[0]].at[right[1]], g_buf.at[slot], g_sem.at[slot]))
            rkeys.append(right)
            fresh_r = True
        else:
            fresh_r = False
        steps.append((u, len(lkeys) - 1, fresh_l, len(rkeys) - 1, fresh_r))
    for copy in lcopies[: deep - 1] + rcopies[: deep - 1]:
        copy.start()
    for u, li, fresh_l, ri, fresh_r in steps:
        if fresh_l:
            lcopies[li].wait()
            if li + deep - 1 < len(lcopies):
                lcopies[li + deep - 1].start()
            x_t[...] = x_buf[li % deep].T
        if fresh_r:
            rcopies[ri].wait()
            if ri + deep - 1 < len(rcopies):
                rcopies[ri + deep - 1].start()
        wide = 2 * LANES

        def tile(n, carry):
            part = nn(x_t[...], g_buf[ri % deep, :, pl.ds(pl.multiple_of(n * wide, wide), wide)])
            for c in range(2):
                rows_scr[pl.ds(u * width * SUBLANES + 2 * n + c, width, stride=SUBLANES), :] = part[
                    :, c * LANES : (c + 1) * LANES
                ]
            return carry

        lax.fori_loop(0, width // wide, tile, 0)

    def block(b, carry):
        slot = lax.rem(b, wide_out)

        def move(q, carry):
            came = [pl.multiple_of(places[b * rows + q * group + j] * SUBLANES, SUBLANES) for j in range(group)]
            held = [rows_scr[pl.ds(first, SUBLANES), :] for first in came]
            for j in range(group):
                to = q * (group // SUBLANES) * TILE + j // SUBLANES * TILE + j % SUBLANES
                stage[pl.ds(to, SUBLANES, stride=SUBLANES), :] = held[j]
            return carry

        lax.fori_loop(0, rows // group, move, 0)

        @pl.when(b >= wide_out)
        def _():
            pltpu.make_async_copy(outbuf.at[slot], out.at[b - wide_out], out_sem.at[slot]).wait()

        for first in range(0, rows, 16):
            tall = min(16, rows - first)
            for c in range(cols):
                at = first * SUBLANES + c * SUBLANES
                both = jnp.concatenate([stage[at : at + SUBLANES, :], stage[at + TILE : at + TILE + SUBLANES, :]], 0)
                outbuf[slot, first : first + tall, c * LANES : (c + 1) * LANES] = both[:tall].astype(BF)
        pltpu.make_async_copy(outbuf.at[slot], out.at[b], out_sem.at[slot]).start()
        return carry

    lax.fori_loop(0, blocks, block, 0)
    for b in range(blocks - wide_out, blocks):
        pltpu.make_async_copy(outbuf.at[b % wide_out], out.at[b], out_sem.at[b % wide_out]).wait()


def weight_grads(role, places, lefts, rights, blocks):
    tokens, width = lefts[0].shape[1:]
    cuts = lefts[-1].shape[0]
    total = places.shape[0]
    rows = total // blocks
    plan = (
        [(("patch", 0), ("de", 0)), (("mixed", 0), ("mid", 0)), (("head", 0), ("pred", 0))]
        + [(("attn", 0), ("dqkv", j)) for j in range(3)]
        + [(("ffn", 0), ("du", j)) for j in range(cuts)]
        + [(("act", j), ("down", 0)) for j in range(cuts)]
    )
    return pl.pallas_call(
        functools.partial(grads_kernel, plan),
        name="weight_grads",
        out_shape=jax.ShapeDtypeStruct((blocks, rows, width), BF),
        in_specs=[smem_spec(), smem_spec()] + [any_spec()] * 12,
        out_specs=any_spec(),
        scratch_shapes=[
            pltpu.VMEM((total * SUBLANES, LANES), F32),
            pltpu.VMEM((4, tokens, width), BF),
            pltpu.VMEM((width, tokens), BF),
            pltpu.VMEM((4, tokens, width), BF),
            pltpu.VMEM((pl.cdiv(rows, 16) * 2 * TILE, LANES), F32),
            pltpu.VMEM((4, rows, width), BF),
            pltpu.SemaphoreType.DMA((4,)),
            pltpu.SemaphoreType.DMA((4,)),
            pltpu.SemaphoreType.DMA((4,)),
        ],
        compiler_params=pltpu.CompilerParams(vmem_limit_bytes=VMEM_LIMIT),
    )(role, places, *lefts, *rights)


def adam_update(weight, first_state, second_state, gradient, step_value, decay_rate):
    first_state = BETA_ONE * first_state + (1.0 - BETA_ONE) * gradient
    second_state = BETA_TWO * second_state + (1.0 - BETA_TWO) * gradient * gradient
    fix_one = 1.0 - jnp.power(BETA_ONE, step_value)
    fix_two = 1.0 - jnp.power(BETA_TWO, step_value)
    update = first_state / fix_one / (jnp.sqrt(second_state / fix_two) + ADAM_EPS)
    return (weight - RATE * (update + decay_rate * weight), first_state, second_state)


def body(
    patches,
    segments,
    positions,
    owners,
    master,
    moment_one,
    moment_two,
    teacher,
    gains,
    gain_one,
    gain_two,
    teacher_gains,
    step_count,
):
    core = lax.axis_index("group")
    width = patches.shape[3]
    slots = patches.shape[2]
    row_total = owners.shape[0]
    inner = (row_total - 6 * width) // 2
    places = piece_rows(owners, width, inner)
    spots = places // SUBLANES * TILE + places % SUBLANES
    chips = lax.axis_size("dp")
    devices = lax.axis_size("group") * chips
    own_rows = row_total // devices
    role = core.astype(jnp.int32).reshape(1)
    place = jnp.stack([core, lax.axis_index("dp")]).astype(jnp.int32)
    listed = jnp.full((1,), MASKED * lax.axis_size("dp") * MICRO_BATCHES, F32)

    both = jnp.stack([teacher, master]).astype(BF)
    if chips <= KERNEL_CHIPS:
        model = gather_weights(both, chips)
    else:
        parts = lax.all_gather(both, ("dp", "group"), axis=1)
        model = jnp.where(core == 1, parts[1], parts[0]).reshape(chips, 2, own_rows, width)
    w = place_weights(spots, model)
    w_far = lax.ppermute(w, "group", [(1, 0)])
    gain_set = jnp.where(core == 1, gains, teacher_gains)
    patch = patches[:, 0]
    seg = segments
    pos = positions
    e, qkv, lse, mixed, x1, x2, tgt, bank = forward(role, patch, seg, pos, gain_set, w)
    (e, qkv, lse, mixed, x1, x2, tgt), banks = exchange_states((e, qkv, lse, mixed, x1, x2, tgt), bank, chips)
    banks = banks.reshape(chips * IMGS, width)
    head, attn, ffn, act, de, mid, pred, dqkv, du, down, small = backward(
        listed, place, seg, pos, gains, lse, banks, e, qkv, x1, x2, tgt, w, w_far
    )
    blocked = weight_grads(
        role, places, (patch, mixed, head, attn, ffn, act), (de, mid, pred, dqkv, du, down), devices
    )
    if chips <= KERNEL_CHIPS:
        owned_grad = reduce_grads(blocked.reshape(2, chips, own_rows, width), chips)
    else:
        owned_grad = lax.psum_scatter(blocked, ("group", "dp"), scatter_dimension=0, tiled=True)
        owned_grad = owned_grad.reshape(own_rows, width).astype(F32)
    square_own = jnp.sum(owned_grad * owned_grad)
    row_id = lax.broadcasted_iota(jnp.int32, small.shape, 0)
    small = sum_tiles(jnp.where(row_id == 5, square_own, small), chips)
    gain_sum, loss_sum, square_sum = small[0:4], small[4, 0], small[5, 0]
    grad_norm = jnp.sqrt(square_sum + jnp.sum(gain_sum * gain_sum))
    factor = jnp.minimum(1.0, CLIP / grad_norm)
    step_value = step_count[0].astype(F32)
    master_new, one_new, two_new = adam_update(
        master, moment_one, moment_two, owned_grad * factor, step_value, DECAY
    )
    gone_new, gtwo_new = adam_update(gains, gain_one, gain_two, gain_sum * factor, step_value, 0.0)[1:]
    teacher_new = EMA_KEEP * teacher + (1.0 - EMA_KEEP) * master_new
    return (
        loss_sum.reshape(1),
        grad_norm.reshape(1),
        one_new,
        two_new,
        master_new,
        teacher_new,
        gone_new,
        gtwo_new,
    )


def solution(mesh):
    rows = P(("group", "dp"), None)
    in_specs = (
        P(None, "dp", None, None),
        P(None, "dp", None),
        P(None, "dp", None),
        P(),
        rows,
        rows,
        rows,
        rows,
        P(),
        P(),
        P(),
        P(),
        P(),
    )
    out_specs = (P(), P(), rows, rows, rows, rows, P(), P())
    return jax.shard_map(body, mesh=mesh, in_specs=in_specs, out_specs=out_specs, check_vma=False)
```

profile of v0, /device:TPU:0, one launch (start us, length us, event | category | flops | bytes accessed | tf_op | source)
XLA Modules:
  0.0 429.1 jit_solution(14196921585189068739)
XLA Ops:
  0.6 1.6 convert_bitcast_fusion
  2.3 1.1 pad_maximum_fusion.both
  3.3 132.6 %gather_weights.1.model = bf16[16,2,336,768]{3,2,1,0:T(8,128)(2,1)} custom-call(bf16[2,336,768]{2,1,0:T(8,128)(2,1)} %pad_maximum_fusion.both), custom_call_target="tpu_custom_call" | custom-call | tf_op jit(solution)/shard_map/gather_weights/pallas_call | solution.py:232
  135.9 1.6 fusion.10
  137.5 29.8 %place_weights.1.w_hbm.w_own = bf16[14,768,768]{2,1,0:T(8,128)(2,1)} custom-call(s32[10752]{0:T(1024)} %get-tuple-element.66.spots, bf16[16,2,336,768]{3,2,1,0:T(8,128)(2,1)} %gather_weights.1.model), custom_call_target="tpu_custom_call" | custom-call | tf_op jit(solution)/shard_map/place_weights/pallas_call | solution.py:624
  167.2 1.3 collective-permute-start
  168.6 0.6 broadcast_select_fusion.1.gain
  169.2 52.9 %forward.1 = (f32[2,512,768]{2,1,0:T(8,128)}, bf16[3,1024,768]{2,1,0:T(8,128)(2,1)}, f32[2,12,512]{2,1,0:T(8,128)}, bf16[2,512,768]{2,1,0:T(8,128)(2,1)}, f32[2,...) custom-call(s32[1]{0:T(128)} %bitcast.role, ...), custom_call_target="tpu_custom_call" | custom-call | flops 16911433728 | bytes 16515072 | tf_op jit(solution)/shard_map/forward/pallas_call | solution.py:750
  222.1 17.1 %exchange_states.1 = (f32[2,512,768]{2,1,0:T(8,128)}, bf16[3,1024,768]{2,1,0:T(8,128)(2,1)}, f32[2,12,512]{2,1,0:T(8,128)}, bf16[2,512,768]{2,1,0:T(8,128)(2,1)}...) custom-call(f32[2,512,768]{2,1,0:T(8,128)} %get-tuple-element.35.ref, ...), custom_call_target="tpu_custom_call", output_to_operand_aliasing={{0}: (0, {}), {1}: (1, {}), {2}: (2, {}), {3}: (3, {}), {4}... | custom-call | tf_op jit(solution)/shard_map/exchange_states/pallas_call | solution.py:484
  239.2 1.6 reshape.38.banks
  241.5 0.6 pad_add_fusion.place
  242.1 0.0 collective-permute-done.w_far
  242.1 44.4 %backward.1 = (bf16[1,512,768]{2,1,0:T(8,128)(2,1)}, bf16[1,512,768]{2,1,0:T(8,128)(2,1)}, bf16[1,512,768]{2,1,0:T(8,128)(2,1)}, bf16[4,512,768]{2,1,0:T(8,128)(...) custom-call(f32[1]{0:T(128)} %constant.106.clone.1.listed, ...), custom_call_target="tpu_custom_call" | custom-call | tf_op jit(solution)/shard_map/backward/pallas_call | solution.py:992
  286.5 39.1 %weight_grads.1 = bf16[32,336,768]{2,1,0:T(8,128)(2,1)} custom-call(s32[1]{0:T(128)} %bitcast.role, s32[10752]{0:T(1024)} %get-tuple-element.67.places, bf16[2,512,768]{2,1,0:T(8,128)(2,1)} %bitcast.15, bf16[2,512,768]{2,1,0:T(8,128)(2,1)} %get-tuple-element.43.mixed, bf16[1,512,768]{2,1,0:T(8,128)(2,1)} %get-tuple-element.51.head, ...), custom_call_target="tpu_custom_call" | custom-call | tf_op jit(solution)/shard_map/weight_grads/pallas_call | solution.py:1120
  325.5 0.0 copy-start.3
  325.6 71.0 %reduce_grads.1 = f32[336,768]{1,0:T(8,128)} custom-call(bf16[2,16,336,768]{3,2,1,0:T(8,128)(2,1)} %bitcast.13), custom_call_target="tpu_custom_call" | custom-call | tf_op jit(solution)/shard_map/reduce_grads/pallas_call | solution.py:374
  396.5 2.1 multiply_reduce_fusion
  398.6 0.0 copy-done.1
  398.6 1.3 broadcast_select_fusion.tile
  400.0 17.4 %sum_tiles.1 = f32[8,768]{1,0:T(8,128)} custom-call(f32[8,768]{1,0:T(8,128)} %broadcast_select_fusion.tile), custom_call_target="tpu_custom_call" | custom-call | tf_op jit(solution)/shard_map/sum_tiles/pallas_call | solution.py:551
  417.4 1.3 fusion.26
  418.7 1.3 multiply_reduce_fusion.1
  421.4 1.4 fusion.23
  422.8 5.0 %multiply_add_fusion = (f32[336,768]{1,0:T(8,128)}, f32[336,768]{1,0:T(8,128)}, f32[336,768]{1,0:T(8,128)}, f32[336,768]{1,0:T(8,128)}) fusion(f32[336,768]{1,0:T(8,128)} %param.20, f32[336,768]{1,0:T(8,128)} %param.17, f32[]{:T(128)} %bitcast.10, f32[]{:T(128)} %bitcast.9, f32[336,768]{1,0:T(8,128)} %reduce_grads.1, f32[]{:T(128)S(6)} %min.3, ...), kind=kLoop, calls=%fused_computation.3 | loop fusion | flops 4902912 | bytes 9289740 | tf_op jit(solution)/shard_map/add | solution.py:1216
  (7 shorter events, 0.0 us)
Async XLA Ops:
  137.5 31.1 %copy-start = (f32[4,768]{1,0:T(4,128)S(1)}, f32[4,768]{1,0:T(4,128)}, u32[]{:S(2)}) copy-start(f32[4,768]{1,0:T(4,128)} %gain.1) | copy-start | bytes 36868
  137.5 31.1 %copy-start.2 = (f32[4,768]{1,0:T(4,128)S(1)}, f32[4,768]{1,0:T(4,128)}, u32[]{:S(2)}) copy-start(f32[4,768]{1,0:T(4,128)} %param.24) | copy-start | bytes 36868
  167.2 74.9 %collective-permute-start = (bf16[14,768,768]{2,1,0:T(8,128)(2,1)}, bf16[14,768,768]{2,1,0:T(8,128)(2,1)}, u32[]{:S(2)}, u32[]{:S(2)}) collective-permute-start(bf16[14,768,768]{2,1,0:T(8,128)(2,1)} %place_weights.1.w_hbm.w_own), channel_id=1, source_target_pairs={{16,0},{17,1},{18,2},{19,3},{20,4},{21,5},{22,6},{23,7},{24,8},{25... | collective-permute-start | bytes 49545224 | tf_op jit(solution)/shard_map/ppermute | solution.py:1186
  325.5 73.1 %copy-start.1 = (f32[8,768]{1,0:T(8,128)S(1)}, f32[8,768]{1,0:T(8,128)}, u32[]{:S(2)}) copy-start(f32[8,768]{1,0:T(8,128)} %get-tuple-element.61) | copy-start | bytes 73732
  325.5 95.8 %copy-start.3 = (f32[4,768]{1,0:T(4,128)S(1)}, f32[4,768]{1,0:T(4,128)}, u32[]{:S(2)}) copy-start(f32[4,768]{1,0:T(4,128)} %param.23) | copy-start | bytes 36868
where the time goes:
time: 433 us; the launch traced here: 429 us
  Pallas kernels  404 us (93%)
  other arithmetic  16.6 us (4%)
    pallas_call x1, Pallas kernels, gather_weights(): pl.pallas_call(functools.partial(gather_kernel, grid), name='gather_weigh...  133 us
    pallas_call x1, Pallas kernels, reduce_grads(): pl.pallas_call(functools.partial(reduce_kernel, grid), name='reduce_grads...  71 us
    pallas_call x1, Pallas kernels, forward(): pl.pallas_call(fwd_kernel, name='forward', grid=(batches,), out_shape=(to...  52.9 us
    pallas_call x1, Pallas kernels, backward(): pl.pallas_call(bwd_kernel, name='backward', out_shape=tuple((jax.ShapeDty...  44.4 us
    pallas_call x1, Pallas kernels, weight_grads(): pl.pallas_call(functools.partial(grads_kernel, plan), name='weight_grads'...  39.1 us
    pallas_call x1, Pallas kernels, place_weights(): pl.pallas_call(place_kernel, name='place_weights', out_shape=jax.ShapeDty...  29.8 us
    pallas_call x1, Pallas kernels, sum_tiles(): pl.pallas_call(functools.partial(sum_kernel, grid), name='sum_tiles', out...  17.4 us
    pallas_call x1, Pallas kernels, exchange_states(): pl.pallas_call(exchange_kernel, name='exchange_states', out_shape=tuple((...  17.1 us
  transfers between devices with their start and end apart: 1, of which 0 were waited for; matrix products, arithmetic and copies ran while one was open for 1% of the time, Pallas kernels for 16%

commit v1 on v0

--- a/solution.py
+++ b/solution.py
@@ -169,14 +169,16 @@
     pl.semaphore_wait(barrier, 1 + sum([1 if there is None else there.astype(jnp.int32) for _, there in near]))
 
 
-def gather_kernel(grid, both, out, swap_sem, send_sem, recv_sem):
+def gather_kernel(grid, learn, teach, out, both, swap_sem, send_sem, recv_sem):
     group, me = lax.axis_index("group"), lax.axis_index("dp")
     coords = coords_of(me, grid)
     routes = lanes_of(both.shape[2])
     events = route_events(grid, routes)
+    both[0] = teach[...].astype(BF)
+    both[1] = learn[...].astype(BF)
+    greet(me, coords, grid, group)
     keep = pltpu.make_async_copy(both.at[group], out.at[me, group], swap_sem.at[2])
     keep.start()
-    greet(me, coords, grid, group)
     swap = pltpu.make_async_remote_copy(
         both.at[1 - group], out.at[me, group], swap_sem.at[0], swap_sem.at[1], {"group": 1 - group}, MESH
     )
@@ -226,16 +228,17 @@
         visit(c, r, finish)
 
 
-def gather_weights(both, chips):
+def gather_weights(learn, teach, chips):
     grid = chip_grid(chips)
-    _, rows, width = both.shape
+    rows, width = learn.shape
     return pl.pallas_call(
         functools.partial(gather_kernel, grid),
         name="gather_weights",
         out_shape=jax.ShapeDtypeStruct((chips, 2, rows, width), BF),
-        in_specs=[pl.BlockSpec(memory_space=pltpu.VMEM)],
+        in_specs=[pl.BlockSpec(memory_space=pltpu.VMEM)] * 2,
         out_specs=any_spec(),
         scratch_shapes=[
+            pltpu.VMEM((2, rows, width), BF),
             pltpu.SemaphoreType.DMA((3,)),
             pltpu.SemaphoreType.DMA((4, slots_of(grid), chips)),
             pltpu.SemaphoreType.DMA((4, chips)),
@@ -243,10 +246,52 @@
         compiler_params=pltpu.CompilerParams(
             collective_id=1, has_side_effects=True, vmem_limit_bytes=VMEM_LIMIT
         ),
-    )(both)
-
-
-def reduce_kernel(grid, blocked, out, acc, heard, load_sem, half_sem, send_sem, recv_sem):
+    )(learn, teach)
+
+
+def sum_peers(group, me, grid):
+    plane = grid[1] * grid[2]
+    at, level = lax.rem(me, plane), me // plane
+    place = (group * plane + at, level)
+    sizes = (2 * plane, grid[0])
+    peers = []
+    for k in range(1, sizes[0]):
+        other = lax.rem(place[0] + k, sizes[0])
+        peers.append((0, k, (other // plane, level * plane + lax.rem(other, plane))))
+    for k in range(1, sizes[1]):
+        peers.append((1, k, (group, lax.rem(level + k, sizes[1]) * plane + at)))
+    return place, sizes, peers
+
+
+def sum_stages(place, sizes, peers, total, notes, note_send, note_recv):
+    for s, size in enumerate(sizes):
+        notes[s, place[s]] = total[...]
+        copies = [
+            pltpu.make_async_remote_copy(
+                notes.at[s, place[s]], notes.at[s, place[s]], note_send.at[s, k], note_recv.at[s, place[s]], device, MESH
+            )
+            for t, k, device in peers
+            if t == s
+        ]
+        for copy in copies:
+            copy.start()
+        for k in range(1, size):
+            other = lax.rem(place[s] + k, size)
+            part = notes.at[s, other]
+            pltpu.make_async_remote_copy(
+                part, part, note_send.at[s, k], note_recv.at[s, other], peers[0][2], MESH
+            ).wait_recv()
+        result = notes[s, 0]
+        for k in range(1, size):
+            result = result + notes[s, k]
+        total[...] = result
+        for copy in copies:
+            copy.wait_send()
+
+
+def reduce_kernel(
+    grid, blocked, small, out, total, acc, heard, notes, load_sem, half_sem, send_sem, recv_sem, note_send, note_recv
+):
     group, me = lax.axis_index("group"), lax.axis_index("dp")
     coords = coords_of(me, grid)
     rows, width = out.shape
@@ -259,7 +304,11 @@
         return tuple(r[routes[c][0].index(d)] for d in range(3))
 
     firsts = list(dict.fromkeys([spot(c, r) for c, r in events]))
-    greet(me, coords, grid, group)
+    place, sizes, peers = sum_peers(group, me, grid)
+    barrier = pltpu.get_barrier_semaphore()
+    for _, _, device in peers:
+        pl.semaphore_signal(barrier, 1, device_id=device, device_id_type=MESH)
+    pl.semaphore_wait(barrier, len(peers))
 
     def load(where, act):
         block, real = origin(me, coords, grid, (0, 1, 2), where)
@@ -360,6 +409,14 @@
             ready.add(spot(c, r))
             load(spot(c, r), load_wait)
         visit(c, r)
+    def squares(k, carry):
+        part = out[pl.ds(pl.multiple_of(k * tall, tall), tall), :]
+        return carry + jnp.sum(part * part, axis=0, keepdims=True)
+
+    square = lax.fori_loop(0, rows // tall, squares, jnp.zeros((1, width), F32))
+    row_id = lax.broadcasted_iota(jnp.int32, total.shape, 0)
+    total[...] = jnp.where(row_id == 5, square, small[...])
+    sum_stages(place, sizes, peers, total, notes, note_send, note_recv)
     for c, r in events:
         if any(r):
             block, real = origin(me, coords, grid, routes[c][0], r)
@@ -368,27 +425,31 @@
         load(where, load_end)
 
 
-def reduce_grads(blocked, chips):
+def reduce_grads(blocked, small, chips):
     grid = chip_grid(chips)
     _, _, rows, width = blocked.shape
+    most = max(grid[0], 2 * grid[1] * grid[2])
     return pl.pallas_call(
         functools.partial(reduce_kernel, grid),
         name="reduce_grads",
-        out_shape=jax.ShapeDtypeStruct((rows, width), F32),
-        in_specs=[any_spec()],
-        out_specs=pl.BlockSpec(memory_space=pltpu.VMEM),
+        out_shape=(jax.ShapeDtypeStruct((rows, width), F32), jax.ShapeDtypeStruct(small.shape, F32)),
+        in_specs=[any_spec(), pl.BlockSpec(memory_space=pltpu.VMEM)],
+        out_specs=(pl.BlockSpec(memory_space=pltpu.VMEM),) * 2,
         scratch_shapes=[
             pltpu.VMEM((chips, rows, width), BF),
             pltpu.VMEM((slots_of(grid) + 1, chips, rows, width), BF),
+            pltpu.VMEM((2, most) + small.shape, F32),
             pltpu.SemaphoreType.DMA((chips,)),
             pltpu.SemaphoreType.DMA((2, chips)),
             pltpu.SemaphoreType.DMA((4, chips)),
             pltpu.SemaphoreType.DMA((4, slots_of(grid), chips)),
+            pltpu.SemaphoreType.DMA((2, most)),
+            pltpu.SemaphoreType.DMA((2, most)),
         ],
         compiler_params=pltpu.CompilerParams(
             collective_id=2, has_side_effects=True, vmem_limit_bytes=VMEM_LIMIT
         ),
-    )(blocked)
+    )(blocked, small)
 
 
 def exchange_kernel(*refs):
@@ -501,68 +562,6 @@
     return outs[:-1], outs[-1]
 
 
-def sum_kernel(grid, tile, out, heard, send_sem, recv_sem):
-    group, me = lax.axis_index("group"), lax.axis_index("dp")
-    coords = coords_of(me, grid)
-    lengths = (2,) + grid
-    mine = (group,) + coords
-    peers = []
-    for s, length in enumerate(lengths):
-        for k in range(1, length):
-            other = lax.rem(mine[s] + k, length)
-            if s == 0:
-                peers.append((s, k, (other, me)))
-            else:
-                peers.append((s, k, (group, me + (other - mine[s]) * strides_of(grid)[s - 1])))
-    barrier = pltpu.get_barrier_semaphore()
-    for _, _, device in peers:
-        pl.semaphore_signal(barrier, 1, device_id=device, device_id_type=MESH)
-    pl.semaphore_wait(barrier, len(peers))
-    out[...] = tile[...]
-    for s, length in enumerate(lengths):
-        if length == 1:
-            continue
-        heard[s, mine[s]] = out[...]
-        copies = [
-            pltpu.make_async_remote_copy(
-                heard.at[s, mine[s]], heard.at[s, mine[s]], send_sem.at[s, k], recv_sem.at[s, mine[s]], device, MESH
-            )
-            for t, k, device in peers
-            if t == s
-        ]
-        for copy in copies:
-            copy.start()
-        for k in range(1, length):
-            other = lax.rem(mine[s] + k, length)
-            pltpu.make_async_remote_copy(
-                heard.at[s, other], heard.at[s, other], send_sem.at[s, k], recv_sem.at[s, other], (group, me), MESH
-            ).wait_recv()
-        total = heard[s, 0]
-        for k in range(1, length):
-            total = total + heard[s, k]
-        out[...] = total
-        for copy in copies:
-            copy.wait_send()
-
-
-def sum_tiles(tile, chips):
-    grid = chip_grid(chips)
-    most = max((2,) + grid)
-    return pl.pallas_call(
-        functools.partial(sum_kernel, grid),
-        name="sum_tiles",
-        out_shape=jax.ShapeDtypeStruct(tile.shape, F32),
-        in_specs=[pl.BlockSpec(memory_space=pltpu.VMEM)],
-        out_specs=pl.BlockSpec(memory_space=pltpu.VMEM),
-        scratch_shapes=[
-            pltpu.VMEM((4, most) + tile.shape, F32),
-            pltpu.SemaphoreType.DMA((4, most)),
-            pltpu.SemaphoreType.DMA((4, most)),
-        ],
-        compiler_params=pltpu.CompilerParams(collective_id=4, has_side_effects=True),
-    )(tile)
-
-
 def place_kernel(spots, model, out, rows_scr, inbuf, stage, outbuf, in_sem, out_sem):
     chips, cores, rows, width = model.shape
     blocks = cores * chips
@@ -666,8 +665,10 @@
     return jnp.where(keep, x, jnp.zeros_like(x))
 
 
-def fwd_kernel(role, patch, seg, pos, gain, w_hbm, e_out, qkv, lse, o_out, x1_out, x2_out, tgt, bank, w, bias, sem):
+def fwd_kernel(patch, seg, pos, gains, teacher_gains, w_hbm, e_out, qkv, lse, o_out, x1_out, x2_out, tgt, bank, w, bias, gain, sem):
     i = pl.program_id(0)
+    role = lax.axis_index("group")
+    gain[...] = jnp.where(role == 0, teacher_gains[...], gains[...])
     slots, width = patch.shape[1:]
     pieces = w_hbm.shape[0]
     cuts = (pieces - 6) // 2
@@ -688,7 +689,7 @@
     seg_row = seg[0]
     seg_col = column_of(seg_row)
     fill_bias(bias, seg_col, seg_row)
-    flags = flag_column(pos[0], slots) * role[0]
+    flags = flag_column(pos[0], slots) * role
     need(0)
     e = nn(patch[0], w[0])
     e = jnp.where(flags > 0, gain[3:4, :], e)
@@ -729,7 +730,7 @@
         acc = acc + nn(act, w[6 + cuts + j])
     x2_out[0] = acc
 
-    @pl.when(role[0] == 0)
+    @pl.when(role == 0)
     def _():
         t = layer_stats(x2_out[0])[0].astype(BF)
         tgt[0] = t
@@ -742,7 +743,7 @@
             bank[0, m : m + 1, :] = unit.astype(BF)
 
 
-def forward(role, patch, seg, pos, gain, w):
+def forward(patch, seg, pos, gains, teacher_gains, w):
     batches, slots, width = patch.shape
     pieces = w.shape[0]
     tok = lambda dt: jax.ShapeDtypeStruct((batches, slots, width), dt)
@@ -762,10 +763,10 @@
             jax.ShapeDtypeStruct((batches, IMGS, width), BF),
         ),
         in_specs=[
-            smem_spec(),
             row,
             pl.BlockSpec((1, 1, slots), lambda i: (i, 0, 0)),
             pl.BlockSpec((1, 1, pos.shape[2]), lambda i: (i, 0, 0)),
+            pl.BlockSpec((4, width), lambda i: (0, 0)),
             pl.BlockSpec((4, width), lambda i: (0, 0)),
             any_spec(),
         ],
@@ -782,13 +783,14 @@
         scratch_shapes=[
             pltpu.VMEM((pieces, width, width), BF),
             pltpu.VMEM((slots, slots), F32),
+            pltpu.VMEM((4, width), F32),
             pltpu.SemaphoreType.DMA((pieces,)),
         ],
         compiler_params=pltpu.CompilerParams(vmem_limit_bytes=VMEM_LIMIT),
         cost_estimate=pl.CostEstimate(
             flops=2 * batches * slots * width * width * pieces, bytes_accessed=2 * w.size, transcendentals=0
         ),
-    )(role, patch, seg, pos, gain, w)
+    )(patch, seg, pos, gains, teacher_gains, w)
 
 
 def norm_back(grad_out, normed, scaled, gain_vec):
@@ -799,13 +801,14 @@
 
 
 def bwd_kernel(
-    listed, place, seg, pos, gain, lse, banks, e_hbm, qkv_hbm, x1_hbm, x2_hbm, tgt_hbm, w_own, w_far,
+    seg, pos, gain, lse, banks, e_hbm, qkv_hbm, x1_hbm, x2_hbm, tgt_hbm, w_own, w_far,
     head_out, attn_out, ffn_out, act_out, de_out, mid_out, pred_out, dqkv_out, du_out, down_out, small,
-    w, bias, top_scr, pool_scr, e_in, qkv, x1_in, x2_in, tgt,
+    w, bias, top_scr, pool_scr, bank_scr, e_in, qkv, x1_in, x2_in, tgt,
     head_v, attn_v, ffn_v, act_v, de_v, mid_v, pred_v, dqkv, du_v, down_v, sem, in_sem, out_sem,
 ):
-    role = place[0]
+    role, chip = lax.axis_index("group"), lax.axis_index("dp")
     slots, width = e_in.shape
+    chips = banks.shape[0]
     pieces = w_own.shape[0]
     cuts = (pieces - 6) // 2
     tokens = pl.ds(pl.multiple_of(role * slots, slots), slots)
@@ -865,7 +868,7 @@
     size = jnp.abs(diff)
     huber = jnp.where(size < 1.0, 0.5 * diff * diff, size - 0.5)
     regress = jnp.sum(jnp.sum(valid * huber, axis=1, keepdims=True), axis=0, keepdims=True)
-    count = listed[0] * width
+    count = float(MASKED * chips * MICRO_BATCHES * width)
     grad_pred = valid * (jnp.clip(diff, -1.0, 1.0) / count)
     pool_scr[...] = jnp.zeros_like(pool_scr)
     for m in range(IMGS):
@@ -875,13 +878,15 @@
     pooled = pool_scr[...]
     length = lax.rsqrt(jnp.sum(pooled * pooled, axis=-1, keepdims=True) + 1e-06)
     unit = pooled * length
-    memory = banks[...]
+    for k in range(chips):
+        bank_scr[k * IMGS : (k + 1) * IMGS, :] = banks[k].astype(F32)
+    memory = bank_scr[...].astype(BF)
     choices = memory.shape[0]
     logits = nt(unit.astype(BF), memory) / SOFTMAX_TEMPER
     row_id = lax.broadcasted_iota(jnp.int32, logits.shape, 0)
     real = row_id < IMGS
     picked = jnp.where(
-        real & (lax.broadcasted_iota(jnp.int32, logits.shape, 1) == place[1] * IMGS + row_id), 1.0, 0.0
+        real & (lax.broadcasted_iota(jnp.int32, logits.shape, 1) == chip * IMGS + row_id), 1.0, 0.0
     )
     peak = jnp.max(logits, axis=-1, keepdims=True)
     ex = jnp.exp(logits - peak)
@@ -982,7 +987,7 @@
         copy.wait()
 
 
-def backward(listed, place, seg, pos, gain, lse, banks, e, qkv, x1, x2, tgt, w_own, w_far):
+def backward(seg, pos, gain, lse, banks, e, qkv, x1, x2, tgt, w_own, w_far):
     _, slots, width = e.shape
     pieces = w_own.shape[0]
     cuts = (pieces - 6) // 2
@@ -994,13 +999,14 @@
         name="backward",
         out_shape=tuple(jax.ShapeDtypeStruct((n, slots, width), BF) for n in counts)
         + (jax.ShapeDtypeStruct((SUBLANES, width), F32),),
-        in_specs=[smem_spec(), smem_spec()] + [vmem] * 5 + [any_spec()] * 7,
+        in_specs=[vmem] * 5 + [any_spec()] * 7,
         out_specs=(any_spec(),) * len(counts) + (vmem,),
         scratch_shapes=[
             pltpu.VMEM((pieces - 1, width, width), BF),
             pltpu.VMEM((slots, slots), F32),
             pltpu.VMEM((slots, width), F32),
             pltpu.VMEM((SUBLANES, width), F32),
+            pltpu.VMEM((banks.shape[0] * IMGS, width), F32),
             tok(1, F32),
             tok(3, BF),
             tok(1, F32),
@@ -1014,11 +1020,11 @@
             pltpu.SemaphoreType.DMA((sum(counts),)),
         ],
         compiler_params=pltpu.CompilerParams(vmem_limit_bytes=VMEM_LIMIT),
-    )(listed, place, seg, pos, gain, lse, banks, e, qkv, x1, x2, tgt, w_own, w_far)
+    )(seg, pos, gain, lse, banks, e, qkv, x1, x2, tgt, w_own, w_far)
 
 
 def grads_kernel(
-    plan, role, places, patch, mixed, head, attn, ffn, act, de, mid, pred, dqkv, du, down, out,
+    plan, places, patch, mixed, head, attn, ffn, act, de, mid, pred, dqkv, du, down, out,
     rows_scr, x_buf, x_t, g_buf, stage, outbuf, x_sem, g_sem, out_sem,
 ):
     blocks, rows, width = out.shape
@@ -1030,7 +1036,7 @@
 
     def left_of(key):
         name, index = key
-        return lefts[name].at[role[0] if name in ("patch", "mixed") else index]
+        return lefts[name].at[lax.axis_index("group") if name in ("patch", "mixed") else index]
 
     lcopies, rcopies = [], []
     lkeys, rkeys = [], []
@@ -1106,7 +1112,7 @@
         pltpu.make_async_copy(outbuf.at[b % wide_out], out.at[b], out_sem.at[b % wide_out]).wait()
 
 
-def weight_grads(role, places, lefts, rights, blocks):
+def weight_grads(places, lefts, rights, blocks):
     tokens, width = lefts[0].shape[1:]
     cuts = lefts[-1].shape[0]
     total = places.shape[0]
@@ -1121,7 +1127,7 @@
         functools.partial(grads_kernel, plan),
         name="weight_grads",
         out_shape=jax.ShapeDtypeStruct((blocks, rows, width), BF),
-        in_specs=[smem_spec(), smem_spec()] + [any_spec()] * 12,
+        in_specs=[smem_spec()] + [any_spec()] * 12,
         out_specs=any_spec(),
         scratch_shapes=[
             pltpu.VMEM((total * SUBLANES, LANES), F32),
@@ -1135,16 +1141,61 @@
             pltpu.SemaphoreType.DMA((4,)),
         ],
         compiler_params=pltpu.CompilerParams(vmem_limit_bytes=VMEM_LIMIT),
-    )(role, places, *lefts, *rights)
-
-
-def adam_update(weight, first_state, second_state, gradient, step_value, decay_rate):
-    first_state = BETA_ONE * first_state + (1.0 - BETA_ONE) * gradient
-    second_state = BETA_TWO * second_state + (1.0 - BETA_TWO) * gradient * gradient
-    fix_one = 1.0 - jnp.power(BETA_ONE, step_value)
-    fix_two = 1.0 - jnp.power(BETA_TWO, step_value)
-    update = first_state / fix_one / (jnp.sqrt(second_state / fix_two) + ADAM_EPS)
-    return (weight - RATE * (update + decay_rate * weight), first_state, second_state)
+    )(places, *lefts, *rights)
+
+
+def power_of(base, exponent):
+    return lax.fori_loop(0, exponent, lambda _, product: product * base, jnp.float32(1.0))
+
+
+def update_kernel(
+    step, total, gains, gone, gtwo, grad, master, one, two, teacher,
+    loss_out, norm_out, one_out, two_out, master_out, teacher_out, gone_out, gtwo_out,
+):
+    gain_grad = total[0:4, :]
+    square = jnp.sum(total[5:6, :], axis=1, keepdims=True)
+    square = square + jnp.sum(jnp.sum(gain_grad * gain_grad, axis=1, keepdims=True), axis=0, keepdims=True)
+    norm = jnp.sqrt(square)
+    factor = jnp.minimum(1.0, CLIP / norm)
+    fix_one = 1.0 - power_of(BETA_ONE, step[0])
+    fix_two = 1.0 - power_of(BETA_TWO, step[0])
+
+    def moments(first, second, gradient):
+        first = BETA_ONE * first + (1.0 - BETA_ONE) * gradient
+        second = BETA_TWO * second + (1.0 - BETA_TWO) * gradient * gradient
+        return first, second
+
+    @pl.when(pl.program_id(0) == 0)
+    def _():
+        loss_out[0] = jnp.sum(total[4:5, 0:1])
+        norm_out[0] = jnp.sum(norm)
+        gone_out[...], gtwo_out[...] = moments(gone[...], gtwo[...], gain_grad * factor)
+
+    first, second = moments(one[...], two[...], grad[...] * factor)
+    change = first / fix_one / (jnp.sqrt(second / fix_two) + ADAM_EPS)
+    weight = master[...]
+    weight = weight - RATE * (change + DECAY * weight)
+    one_out[...] = first
+    two_out[...] = second
+    master_out[...] = weight
+    teacher_out[...] = EMA_KEEP * teacher[...] + (1.0 - EMA_KEEP) * weight
+
+
+def update(step, total, gains, gone, gtwo, grad, master, one, two, teacher):
+    rows, width = grad.shape
+    tall = max([t for t in range(SUBLANES, 113, SUBLANES) if rows % t == 0], default=rows)
+    part = pl.BlockSpec((tall, width), lambda i: (i, 0))
+    whole = lambda a: pl.BlockSpec(a.shape, lambda i: (0, 0))
+    scalar = jax.ShapeDtypeStruct((1,), F32)
+    same = lambda a: jax.ShapeDtypeStruct(a.shape, F32)
+    return pl.pallas_call(
+        update_kernel,
+        name="update",
+        grid=(rows // tall,),
+        out_shape=(scalar, scalar, same(one), same(two), same(master), same(teacher), same(gone), same(gtwo)),
+        in_specs=[smem_spec(), whole(total), whole(gains), whole(gone), whole(gtwo)] + [part] * 5,
+        out_specs=(smem_spec(), smem_spec(), part, part, part, part, whole(gone), whole(gtwo)),
+    )(step, total, gains, gone, gtwo, grad, master, one, two, teacher)
 
 
 def body(
@@ -1172,57 +1223,35 @@
     chips = lax.axis_size("dp")
     devices = lax.axis_size("group") * chips
     own_rows = row_total // devices
-    role = core.astype(jnp.int32).reshape(1)
-    place = jnp.stack([core, lax.axis_index("dp")]).astype(jnp.int32)
-    listed = jnp.full((1,), MASKED * lax.axis_size("dp") * MICRO_BATCHES, F32)
-
-    both = jnp.stack([teacher, master]).astype(BF)
+
     if chips <= KERNEL_CHIPS:
-        model = gather_weights(both, chips)
+        model = gather_weights(master, teacher, chips)
     else:
-        parts = lax.all_gather(both, ("dp", "group"), axis=1)
+        parts = lax.all_gather(jnp.stack([teacher, master]).astype(BF), ("dp", "group"), axis=1)
         model = jnp.where(core == 1, parts[1], parts[0]).reshape(chips, 2, own_rows, width)
     w = place_weights(spots, model)
     w_far = lax.ppermute(w, "group", [(1, 0)])
-    gain_set = jnp.where(core == 1, gains, teacher_gains)
     patch = patches[:, 0]
     seg = segments
     pos = positions
-    e, qkv, lse, mixed, x1, x2, tgt, bank = forward(role, patch, seg, pos, gain_set, w)
+    e, qkv, lse, mixed, x1, x2, tgt, bank = forward(patch, seg, pos, gains, teacher_gains, w)
     (e, qkv, lse, mixed, x1, x2, tgt), banks = exchange_states((e, qkv, lse, mixed, x1, x2, tgt), bank, chips)
-    banks = banks.reshape(chips * IMGS, width)
     head, attn, ffn, act, de, mid, pred, dqkv, du, down, small = backward(
-        listed, place, seg, pos, gains, lse, banks, e, qkv, x1, x2, tgt, w, w_far
+        seg, pos, gains, lse, banks, e, qkv, x1, x2, tgt, w, w_far
     )
     blocked = weight_grads(
-        role, places, (patch, mixed, head, attn, ffn, act), (de, mid, pred, dqkv, du, down), devices
+        places, (patch, mixed, head, attn, ffn, act), (de, mid, pred, dqkv, du, down), devices
     )
     if chips <= KERNEL_CHIPS:
-        owned_grad = reduce_grads(blocked.reshape(2, chips, own_rows, width), chips)
+        owned_grad, total = reduce_grads(blocked.reshape(2, chips, own_rows, width), small, chips)
     else:
         owned_grad = lax.psum_scatter(blocked, ("group", "dp"), scatter_dimension=0, tiled=True)
         owned_grad = owned_grad.reshape(own_rows, width).astype(F32)
-    square_own = jnp.sum(owned_grad * owned_grad)
-    row_id = lax.broadcasted_iota(jnp.int32, small.shape, 0)
-    small = sum_tiles(jnp.where(row_id == 5, square_own, small), chips)
-    gain_sum, loss_sum, square_sum = small[0:4], small[4, 0], small[5, 0]
-    grad_norm = jnp.sqrt(square_sum + jnp.sum(gain_sum * gain_sum))
-    factor = jnp.minimum(1.0, CLIP / grad_norm)
-    step_value = step_count[0].astype(F32)
-    master_new, one_new, two_new = adam_update(
-        master, moment_one, moment_two, owned_grad * factor, step_value, DECAY
-    )
-    gone_new, gtwo_new = adam_update(gains, gain_one, gain_two, gain_sum * factor, step_value, 0.0)[1:]
-    teacher_new = EMA_KEEP * teacher + (1.0 - EMA_KEEP) * master_new
-    return (
-        loss_sum.reshape(1),
-        grad_norm.reshape(1),
-        one_new,
-        two_new,
-        master_new,
-        teacher_new,
-        gone_new,
-        gtwo_new,
+        squares = jnp.sum(owned_grad * owned_grad, axis=0, keepdims=True)
+        row_id = lax.broadcasted_iota(jnp.int32, small.shape, 0)
+        total = lax.psum(jnp.where(row_id == 5, squares, small), ("group", "dp"))
+    return update(
+        step_count, total, gains, gain_one, gain_two, owned_grad, master, moment_one, moment_two, teacher
     )
 
 

time: 433 us -> 414 us (0.956)
  other arithmetic: 16.6 us -> 1.56 us
    pallas_call x1, Pallas kernels: 71 us -> 83.8 us  [reduce_grads(): pl.pallas_call(functools.partial(reduce_kernel, grid), name='reduce_grads...]
    pallas_call x1, Pallas kernels: 17.4 us -> 5.88 us  [update(): pl.pallas_call(update_kernel, name='update', grid=(rows // tall,), out_sh...]
    add x2 -> x0, other arithmetic: 6.38 us -> none  [the longest x1 5.02 us: body(): teacher_new = EMA_KEEP * teacher + (1.0 - EMA_KEEP) * master_new]
  transfers between devices with their start and end apart: 1 -> 1, of which waited for: 0 -> 0; matrix products, arithmetic and copies ran while one was open for 1% -> 0% of each run, Pallas kernels for 16% -> 17%
where the time goes in v1:
time: 414 us; the launch traced here: 411 us
  Pallas kernels  406 us (98%)
    pallas_call x1, Pallas kernels, gather_weights(): pl.pallas_call(functools.partial(gather_kernel, grid), name='gather_weigh...  133 us
    pallas_call x1, Pallas kernels, reduce_grads(): pl.pallas_call(functools.partial(reduce_kernel, grid), name='reduce_grads...  83.8 us
    pallas_call x1, Pallas kernels, forward(): pl.pallas_call(fwd_kernel, name='forward', grid=(batches,), out_shape=(to...  52.9 us
    pallas_call x1, Pallas kernels, backward(): pl.pallas_call(bwd_kernel, name='backward', out_shape=tuple((jax.ShapeDty...  44.4 us
    pallas_call x1, Pallas kernels, weight_grads(): pl.pallas_call(functools.partial(grads_kernel, plan), name='weight_grads'...  39.8 us
    pallas_call x1, Pallas kernels, place_weights(): pl.pallas_call(place_kernel, name='place_weights', out_shape=jax.ShapeDty...  29.6 us
    pallas_call x1, Pallas kernels, exchange_states(): pl.pallas_call(exchange_kernel, name='exchange_states', out_shape=tuple((...  17.1 us
  transfers between devices with their start and end apart: 1, of which 0 were waited for; matrix products, arithmetic and copies ran while one was open for 0% of the time, Pallas kernels for 17%

profile of v1, /device:TPU:0, one launch (start us, length us, event | category | flops | bytes accessed | tf_op | source)
XLA Modules:
  0.0 410.9 jit_solution(18031948445846043202)
XLA Ops:
  0.6 1.6 fusion.9
  2.2 133.0 %gather_weights.1.model = bf16[16,2,336,768]{3,2,1,0:T(8,128)(2,1)} custom-call(f32[336,768]{1,0:T(8,128)} %master.1, f32[336,768]{1,0:T(8,128)} %teacher.1), custom_call_target="tpu_custom_call" | custom-call | tf_op jit(solution)/shard_map/gather_weights/pallas_call | solution.py:234
  135.2 29.6 %place_weights.1.w_hbm.w_own = bf16[14,768,768]{2,1,0:T(8,128)(2,1)} custom-call(s32[10752]{0:T(1024)} %get-tuple-element.66.spots, bf16[16,2,336,768]{3,2,1,0:T(8,128)(2,1)} %gather_weights.1.model), custom_call_target="tpu_custom_call" | custom-call | tf_op jit(solution)/shard_map/place_weights/pallas_call | solution.py:623
  164.8 1.3 collective-permute-start
  166.8 52.9 %forward.1 = (f32[2,512,768]{2,1,0:T(8,128)}, bf16[3,1024,768]{2,1,0:T(8,128)(2,1)}, f32[2,12,512]{2,1,0:T(8,128)}, bf16[2,512,768]{2,1,0:T(8,128)(2,1)}, f32[2,...) custom-call(bf16[2,512,768]{2,1,0:T(8,128)(2,1)} %bitcast.3, ...), custom_call_target="tpu_custom_call" | custom-call | flops 16911433728 | bytes 16515072 | tf_op jit(solution)/shard_map/forward/pallas_call | solution.py:751
  219.7 17.1 %exchange_states.1 = (f32[2,512,768]{2,1,0:T(8,128)}, bf16[3,1024,768]{2,1,0:T(8,128)(2,1)}, f32[2,12,512]{2,1,0:T(8,128)}, bf16[2,512,768]{2,1,0:T(8,128)(2,1)}...) custom-call(f32[2,512,768]{2,1,0:T(8,128)} %get-tuple-element.37.ref, ...), custom_call_target="tpu_custom_call", output_to_operand_aliasing={{0}: (0, {}), {1}: (1, {}), {2}: (2, {}), {3}: (3, {}), {4}... | custom-call | tf_op jit(solution)/shard_map/exchange_states/pallas_call | solution.py:545
  236.8 0.0 collective-permute-done.w_far
  236.8 44.4 %backward.1 = (bf16[1,512,768]{2,1,0:T(8,128)(2,1)}, bf16[1,512,768]{2,1,0:T(8,128)(2,1)}, bf16[1,512,768]{2,1,0:T(8,128)(2,1)}, bf16[4,512,768]{2,1,0:T(8,128)(...) custom-call(s32[2,1,512]{2,1,0:T(1,128)} %seg.3, ...), custom_call_target="tpu_custom_call" | custom-call | tf_op jit(solution)/shard_map/backward/pallas_call | solution.py:997
  281.2 39.8 %weight_grads.1 = bf16[32,336,768]{2,1,0:T(8,128)(2,1)} custom-call(s32[10752]{0:T(1024)} %get-tuple-element.67.places, bf16[2,512,768]{2,1,0:T(8,128)(2,1)} %bitcast.4, bf16[2,512,768]{2,1,0:T(8,128)(2,1)} %get-tuple-element.45.mixed, bf16[1,512,768]{2,1,0:T(8,128)(2,1)} %get-tuple-element.53.head, bf16[1,512,768]{2,1,0:T(8,128)(2,1)} %get-tuple-element.54.attn, ...), custom_call_target="tpu_custom_call" | custom-call | tf_op jit(solution)/shard_map/weight_grads/pallas_call | solution.py:1126
  321.0 83.8 %reduce_grads.1 = (f32[336,768]{1,0:T(8,128)}, f32[8,768]{1,0:T(8,128)}) custom-call(bf16[2,16,336,768]{3,2,1,0:T(8,128)(2,1)} %bitcast.2, f32[8,768]{1,0:T(8,128)} %get-tuple-element.63.small), custom_call_target="tpu_custom_call" | custom-call | tf_op jit(solution)/shard_map/reduce_grads/pallas_call | solution.py:432
  404.8 5.9 %update.1 = (f32[1]{0:T(128)}, f32[1]{0:T(128)}, f32[336,768]{1,0:T(8,128)}, f32[336,768]{1,0:T(8,128)}, f32[336,768]{1,0:T(8,128)}, /*index=5*/f32[336,768]{1,0:T(8,128)}, f32[4,768]{1,0:T(4,128)}, f32[4,768]{1,0:T(4,128)}) custom-call(s32[1]{0:T(128)S(6)} %copy.35.step, f32[8,768]{1,0:T(8,128)} %get-tuple-element.64.total, f32[4,768]{1,0:T(4,128)} %gains.3, ...), custom_call_target="tpu_custom_call" | custom-call | tf_op jit(solution)/shard_map/update/pallas_call | solution.py:1191
Async XLA Ops:
  164.8 72.0 %collective-permute-start = (bf16[14,768,768]{2,1,0:T(8,128)(2,1)}, bf16[14,768,768]{2,1,0:T(8,128)(2,1)}, u32[]{:S(2)}, u32[]{:S(2)}) collective-permute-start(bf16[14,768,768]{2,1,0:T(8,128)(2,1)} %place_weights.1.w_hbm.w_own), channel_id=1, source_target_pairs={{16,0},{17,1},{18,2},{19,3},{20,4},{21,5},{22,6},{23,7},{24,8},{25... | collective-permute-start | bytes 49545224 | tf_op jit(solution)/shard_map/ppermute | solution.py:1233

commit v2 on v1

--- a/solution.py
+++ b/solution.py
@@ -169,7 +169,7 @@
     pl.semaphore_wait(barrier, 1 + sum([1 if there is None else there.astype(jnp.int32) for _, there in near]))
 
 
-def gather_kernel(grid, learn, teach, out, both, swap_sem, send_sem, recv_sem):
+def gather_kernel(grid, learn, teach, out, both, swap_sem, half_sem, send_sem, recv_sem):
     group, me = lax.axis_index("group"), lax.axis_index("dp")
     coords = coords_of(me, grid)
     routes = lanes_of(both.shape[2])
@@ -183,8 +183,28 @@
         both.at[1 - group], out.at[me, group], swap_sem.at[0], swap_sem.at[1], {"group": 1 - group}, MESH
     )
     swap.start()
-    keep.wait()
+
+    def first_sends(half, source):
+        copies = []
+        for c, (order, first, wide) in enumerate(routes):
+            for d, sign in onward(grid, order, (0, 0, 0)):
+                index, there = neighbour(me, coords, grid, d, sign)
+                copy = pltpu.make_async_remote_copy(
+                    source.at[:, first : first + wide],
+                    out.at[me, half, :, first : first + wide],
+                    half_sem.at[half, c, slot_of(grid, d, sign)],
+                    recv_sem.at[c, me],
+                    {"dp": index},
+                    MESH,
+                )
+                copies.append((there, copy))
+        for there, copy in copies:
+            guarded([there], copy.start)
+        return copies
+
+    firsts = first_sends(group, both.at[group])
     swap.wait()
+    firsts += first_sends(1 - group, out.at[me, 1 - group])
 
     def visit(c, r, act):
         order, first, wide = routes[c]
@@ -208,24 +228,28 @@
                         ),
                     )
                 )
-            act(part, recv_sem.at[c, block], any(r), copies)
+            act(part, recv_sem.at[c, block], copies)
 
         guarded(real, run)
 
-    def forward_on(part, arrival_sem, remote, copies):
-        if remote:
-            pltpu.make_async_remote_copy(part, part, swap_sem.at[0], arrival_sem, {"dp": me}, MESH).wait_recv()
+    def forward_on(part, arrival_sem, copies):
+        pltpu.make_async_remote_copy(part, part, swap_sem.at[0], arrival_sem, {"dp": me}, MESH).wait_recv()
         for there, copy in copies:
             guarded([there], copy.start)
 
-    def finish(part, arrival_sem, remote, copies):
+    def finish(part, arrival_sem, copies):
         for there, copy in copies:
             guarded([there], copy.wait_send)
 
     for c, r in events:
-        visit(c, r, forward_on)
+        if any(r):
+            visit(c, r, forward_on)
     for c, r in events:
-        visit(c, r, finish)
+        if any(r):
+            visit(c, r, finish)
+    keep.wait()
+    for there, copy in firsts:
+        guarded([there], copy.wait_send)
 
 
 def gather_weights(learn, teach, chips):
@@ -240,6 +264,7 @@
         scratch_shapes=[
             pltpu.VMEM((2, rows, width), BF),
             pltpu.SemaphoreType.DMA((3,)),
+            pltpu.SemaphoreType.DMA((2, 4, slots_of(grid))),
             pltpu.SemaphoreType.DMA((4, slots_of(grid), chips)),
             pltpu.SemaphoreType.DMA((4, chips)),
         ],
@@ -665,11 +690,15 @@
     return jnp.where(keep, x, jnp.zeros_like(x))
 
 
-def fwd_kernel(patch, seg, pos, gains, teacher_gains, w_hbm, e_out, qkv, lse, o_out, x1_out, x2_out, tgt, bank, w, bias, gain, sem):
+def fwd_kernel(
+    patch, seg, pos, gains, teacher_gains, w_hbm,
+    e_out, qkv_out, lse_out, o_out, x1_out, x2_out, tgt_out, bank_out,
+    w, bias, gain, a2, e_v, qkv, lse, o_v, x1_v, x2_v, tgt, bank, sem, out_sem,
+):
     i = pl.program_id(0)
     role = lax.axis_index("group")
     gain[...] = jnp.where(role == 0, teacher_gains[...], gains[...])
-    slots, width = patch.shape[1:]
+    batches, slots, width = e_out.shape
     pieces = w_hbm.shape[0]
     cuts = (pieces - 6) // 2
     order = [0, 3, 4, 5, 1]
@@ -685,6 +714,20 @@
         @pl.when(i == 0)
         def _():
             pltpu.make_async_copy(w_hbm.at[u], w.at[u], sem.at[u]).wait()
+
+    def leave(k, b):
+        tokens = pl.ds(pl.multiple_of(b * slots, slots), slots)
+        source, target = [
+            (e_v.at[b], e_out.at[b]),
+            (qkv.at[b], qkv_out.at[:, tokens, :]),
+            (lse.at[b], lse_out.at[b]),
+            (o_v.at[b], o_out.at[b]),
+            (x1_v.at[b], x1_out.at[b]),
+            (x2_v.at[b], x2_out.at[b]),
+            (tgt.at[b], tgt_out.at[b]),
+            (bank.at[b], bank_out.at[b]),
+        ][k]
+        return pltpu.make_async_copy(source, target, out_sem.at[b, k])
 
     seg_row = seg[0]
     seg_col = column_of(seg_row)
@@ -693,15 +736,21 @@
     need(0)
     e = nn(patch[0], w[0])
     e = jnp.where(flags > 0, gain[3:4, :], e)
-    e_out[0] = e
-    a = (layer_stats(e)[0] * gain[0:1, :]).astype(BF)
-    for j in range(3):
+    e_v[i] = e
+    leave(0, i).start()
+    a2[...] = (layer_stats(e)[0] * gain[0:1, :]).astype(BF)
+
+    def project(j, carry):
         need(3 + j)
-        qkv[j] = nn(a, w[3 + j]).astype(BF)
+        qkv[i, j] = nn(a2[...], w[3 + j]).astype(BF)
+        return carry
+
+    lax.fori_loop(0, 3, project, 0)
+    leave(1, i).start()
 
     def pair(p, carry):
         cs = pl.ds(pl.multiple_of(p * LANES, LANES), LANES)
-        q2, k2, v2 = qkv[0, :, cs], qkv[1, :, cs], qkv[2, :, cs]
+        q2, k2, v2 = qkv[i, 0, :, cs], qkv[i, 1, :, cs], qkv[i, 2, :, cs]
         k2 = k2 * jnp.asarray(HEAD_DIM**-0.5, BF)
         v_t = v2.T
         outs = []
@@ -710,81 +759,100 @@
             top = jnp.max(s, axis=0, keepdims=True)
             ex = jnp.exp(s - top)
             total = jnp.sum(ex, axis=0, keepdims=True)
-            lse[0, pl.ds(2 * p + h, 1), :] = top + jnp.log(total)
+            lse[i, pl.ds(2 * p + h, 1), :] = top + jnp.log(total)
             probs = (ex * (1.0 / total)).astype(BF)
             outs.append(nn(v_t[h * HEAD_DIM : (h + 1) * HEAD_DIM, :], probs))
-        o_out[0, :, cs] = jnp.concatenate(outs, axis=0).T.astype(BF)
+        o_v[i, :, cs] = jnp.concatenate(outs, axis=0).T.astype(BF)
         return carry
 
     lax.fori_loop(0, HEADS // 2, pair, 0)
+    leave(2, i).start()
+    leave(3, i).start()
     need(1)
-    x1 = e_out[0] + nn(o_out[0], w[1])
-    x1_out[0] = x1
-    a2 = (layer_stats(x1)[0] * gain[1:2, :]).astype(BF)
-    acc = x1
-    for j in range(cuts):
+    x1 = e_v[i] + nn(o_v[i], w[1])
+    x1_v[i] = x1
+    leave(4, i).start()
+    a2[...] = (layer_stats(x1)[0] * gain[1:2, :]).astype(BF)
+    x2_v[i] = x1
+
+    def ffn(j, carry):
         need(6 + j)
-        hid = nn(a2, w[6 + j])
+        hid = nn(a2[...], w[6 + j])
         act = (hid * (0.5 * (1.0 + jnp.tanh(GELU_A * (hid + GELU_B * hid * hid * hid))))).astype(BF)
         need(6 + cuts + j)
-        acc = acc + nn(act, w[6 + cuts + j])
-    x2_out[0] = acc
+        x2_v[i] += nn(act, w[6 + cuts + j])
+        return carry
+
+    lax.fori_loop(0, cuts, ffn, 0)
+    leave(5, i).start()
 
     @pl.when(role == 0)
     def _():
-        t = layer_stats(x2_out[0])[0].astype(BF)
-        tgt[0] = t
+        t = layer_stats(x2_v[i])[0].astype(BF)
+        tgt[i] = t
+        leave(6, i).start()
         t = t.astype(F32)
         for m in range(IMGS):
             inside = seg_col == m
             size = jnp.sum(jnp.where(inside, 1.0, 0.0), axis=0, keepdims=True)
             pooled = jnp.sum(jnp.where(inside, t, 0.0), axis=0, keepdims=True) / size
             unit = pooled * lax.rsqrt(jnp.sum(pooled * pooled, axis=-1, keepdims=True) + 1e-06)
-            bank[0, m : m + 1, :] = unit.astype(BF)
+            bank[i, m : m + 1, :] = unit.astype(BF)
+        leave(7, i).start()
+
+    @pl.when(i == batches - 1)
+    def _():
+        for b in range(batches):
+            for k in range(6):
+                leave(k, b).wait()
+
+        @pl.when(role == 0)
+        def _():
+            for b in range(batches):
+                leave(6, b).wait()
+                leave(7, b).wait()
 
 
 def forward(patch, seg, pos, gains, teacher_gains, w):
     batches, slots, width = patch.shape
     pieces = w.shape[0]
-    tok = lambda dt: jax.ShapeDtypeStruct((batches, slots, width), dt)
-    row = pl.BlockSpec((1, slots, width), lambda i: (i, 0, 0))
+    tok = lambda n, dt: ((batches,) + ((3,) if n == 3 else ()) + (slots, width), dt)
+    kinds = [
+        tok(1, F32),
+        tok(3, BF),
+        ((batches, HEADS, slots), F32),
+        tok(1, BF),
+        tok(1, F32),
+        tok(1, F32),
+        tok(1, BF),
+        ((batches, IMGS, width), BF),
+    ]
+    outs = [jax.ShapeDtypeStruct(shape, dt) for shape, dt in kinds]
+    outs[1] = jax.ShapeDtypeStruct((3, batches * slots, width), BF)
     return pl.pallas_call(
         fwd_kernel,
         name="forward",
         grid=(batches,),
-        out_shape=(
-            tok(F32),
-            jax.ShapeDtypeStruct((3, batches * slots, width), BF),
-            jax.ShapeDtypeStruct((batches, HEADS, slots), F32),
-            tok(BF),
-            tok(F32),
-            tok(F32),
-            tok(BF),
-            jax.ShapeDtypeStruct((batches, IMGS, width), BF),
-        ),
+        out_shape=tuple(outs),
         in_specs=[
-            row,
+            pl.BlockSpec((1, slots, width), lambda i: (i, 0, 0)),
             pl.BlockSpec((1, 1, slots), lambda i: (i, 0, 0)),
             pl.BlockSpec((1, 1, pos.shape[2]), lambda i: (i, 0, 0)),
             pl.BlockSpec((4, width), lambda i: (0, 0)),
             pl.BlockSpec((4, width), lambda i: (0, 0)),
             any_spec(),
         ],
-        out_specs=(
-            row,
-            pl.BlockSpec((3, slots, width), lambda i: (0, i, 0)),
-            pl.BlockSpec((1, HEADS, slots), lambda i: (i, 0, 0)),
-            row,
-            row,
-            row,
-            row,
-            pl.BlockSpec((1, IMGS, width), lambda i: (i, 0, 0)),
-        ),
+        out_specs=(any_spec(),) * len(outs),
         scratch_shapes=[
             pltpu.VMEM((pieces, width, width), BF),
             pltpu.VMEM((slots, slots), F32),
             pltpu.VMEM((4, width), F32),
+            pltpu.VMEM((slots, width), BF),
+        ]
+        + [pltpu.VMEM(shape, dt) for shape, dt in kinds]
+        + [
             pltpu.SemaphoreType.DMA((pieces,)),
+            pltpu.SemaphoreType.DMA((batches, len(kinds))),
         ],
         compiler_params=pltpu.CompilerParams(vmem_limit_bytes=VMEM_LIMIT),
         cost_estimate=pl.CostEstimate(
@@ -803,7 +871,7 @@
 def bwd_kernel(
     seg, pos, gain, lse, banks, e_hbm, qkv_hbm, x1_hbm, x2_hbm, tgt_hbm, w_own, w_far,
     head_out, attn_out, ffn_out, act_out, de_out, mid_out, pred_out, dqkv_out, du_out, down_out, small,
-    w, bias, top_scr, pool_scr, bank_scr, e_in, qkv, x1_in, x2_in, tgt,
+    w, bias, top_scr, acc_scr, pool_scr, bank_scr, e_in, qkv, x1_in, x2_in, tgt,
     head_v, attn_v, ffn_v, act_v, de_v, mid_v, pred_v, dqkv, du_v, down_v, sem, in_sem, out_sem,
 ):
     role, chip = lax.axis_index("group"), lax.axis_index("dp")
@@ -918,23 +986,35 @@
     ffn_in = (n2 * gain[1:2, :]).astype(BF)
     ffn_v[...] = ffn_in
     keep(ffn_v, ffn_out.at[0])
-    acc = None
-    for j in range(cuts):
+    acc_scr[...] = jnp.zeros_like(acc_scr)
+    loop_sem = len(taken)
+
+    def leave(j):
+        return (
+            pltpu.make_async_copy(act_v.at[j], act_out.at[j], out_sem.at[loop_sem + 2 * j]),
+            pltpu.make_async_copy(du_v.at[j], du_out.at[j], out_sem.at[loop_sem + 2 * j + 1]),
+        )
+
+    def ffn(j, carry):
         need(6 + cuts + j)
-        grad_act = nt(down, w[5 + cuts + j])
+        grad_act = nt(down_v[...], w[5 + cuts + j])
         need(6 + j)
-        hid = nn(ffn_in, w[5 + j])
+        hid = nn(ffn_v[...], w[5 + j])
         th = jnp.tanh(GELU_A * (hid + GELU_B * hid * hid * hid))
         cdf = 0.5 * (1.0 + th)
         act_v[j] = (hid * cdf).astype(BF)
-        keep(act_v.at[j], act_out.at[j])
         slope = cdf + hid * (0.5 * (1.0 - th * th)) * (GELU_A * (1.0 + 3.0 * GELU_B * hid * hid))
         du = (grad_act * slope).astype(BF)
         du_v[j] = du
-        keep(du_v.at[j], du_out.at[j])
-        part = nt(du, w[5 + j])
-        acc = part if acc is None else acc + part
-    grad_ffn, gain_two = norm_back(acc, n2, r2, gain[1:2, :])
+        for copy in leave(j):
+            copy.start()
+        acc_scr[...] += nt(du, w[5 + j])
+        return carry
+
+    lax.fori_loop(0, cuts, ffn, 0)
+    for j in range(cuts):
+        taken.extend(leave(j))
+    grad_ffn, gain_two = norm_back(acc_scr[...], n2, r2, gain[1:2, :])
     small[1:2, :] += gain_two
     mid = top_scr[...] + grad_ffn
     top_scr[...] = mid
@@ -967,16 +1047,19 @@
 
     lax.fori_loop(0, HEADS // 2, pair, 0)
     keep(dqkv, dqkv_out)
-    acc = None
-    for j in range(3):
+    acc_scr[...] = jnp.zeros_like(acc_scr)
+
+    def project(j, carry):
         need(3 + j)
-        part = nt(dqkv[j], w[2 + j])
-        acc = part if acc is None else acc + part
+        acc_scr[...] += nt(dqkv[j], w[2 + j])
+        return carry
+
+    lax.fori_loop(0, 3, project, 0)
     e_copy.wait()
     n1, r1 = layer_stats(e_in[...])
     attn_v[...] = (n1 * gain[0:1, :]).astype(BF)
     keep(attn_v, attn_out.at[0])
-    grad_attn, gain_one = norm_back(acc, n1, r1, gain[0:1, :])
+    grad_attn, gain_one = norm_back(acc_scr[...], n1, r1, gain[0:1, :])
     small[0:1, :] += gain_one
     start = top_scr[...] + grad_attn
     hidden_slot = flags > 0
@@ -1004,6 +1087,7 @@
         scratch_shapes=[
             pltpu.VMEM((pieces - 1, width, width), BF),
             pltpu.VMEM((slots, slots), F32),
+            pltpu.VMEM((slots, width), F32),
             pltpu.VMEM((slots, width), F32),
             pltpu.VMEM((SUBLANES, width), F32),
             pltpu.VMEM((banks.shape[0] * IMGS, width), F32),

time: 414 us -> 403 us (0.973)
  Pallas kernels: 406 us -> 398 us
    pallas_call x1, Pallas kernels: 52.9 us -> 48.4 us  [forward(): pl.pallas_call(fwd_kernel, name='forward', grid=(batches,), out_shape=tup...]
  transfers between devices with their start and end apart: 1 -> 1, of which waited for: 0 -> 0; matrix products, arithmetic and copies ran while one was open for 0% -> 0% of each run, Pallas kernels for 17% -> 16%
where the time goes in v2:
time: 403 us
  Pallas kernels  398 us (99%)
    pallas_call x1, Pallas kernels, gather_weights(): pl.pallas_call(functools.partial(gather_kernel, grid), name='gather_weigh...  130 us
    pallas_call x1, Pallas kernels, reduce_grads(): pl.pallas_call(functools.partial(reduce_kernel, grid), name='reduce_grads...  83.9 us
    pallas_call x1, Pallas kernels, forward(): pl.pallas_call(fwd_kernel, name='forward', grid=(batches,), out_shape=tup...  48.4 us
    pallas_call x1, Pallas kernels, backward(): pl.pallas_call(bwd_kernel, name='backward', out_shape=tuple((jax.ShapeDty...  43.3 us
    pallas_call x1, Pallas kernels, weight_grads(): pl.pallas_call(functools.partial(grads_kernel, plan), name='weight_grads'...  39.9 us
    pallas_call x1, Pallas kernels, place_weights(): pl.pallas_call(place_kernel, name='place_weights', out_shape=jax.ShapeDty...  29.6 us
    pallas_call x1, Pallas kernels, exchange_states(): pl.pallas_call(exchange_kernel, name='exchange_states', out_shape=tuple((...  17.9 us
  transfers between devices with their start and end apart: 1, of which 0 were waited for; matrix products, arithmetic and copies ran while one was open for 0% of the time, Pallas kernels for 16%

profile of v2, /device:TPU:0, one launch (start us, length us, event | category | flops | bytes accessed | tf_op | source)
XLA Modules:
  0.0 402.9 jit_solution(15405617943809386717)
XLA Ops:
  0.6 1.6 fusion.9
  2.2 129.7 %gather_weights.1.model = bf16[16,2,336,768]{3,2,1,0:T(8,128)(2,1)} custom-call(f32[336,768]{1,0:T(8,128)} %master.1, f32[336,768]{1,0:T(8,128)} %teacher.1), custom_call_target="tpu_custom_call" | custom-call | tf_op jit(solution)/shard_map/gather_weights/pallas_call | solution.py:258
  131.9 29.6 %place_weights.1.w_hbm.w_own = bf16[14,768,768]{2,1,0:T(8,128)(2,1)} custom-call(s32[10752]{0:T(1024)} %get-tuple-element.66.spots, bf16[16,2,336,768]{3,2,1,0:T(8,128)(2,1)} %gather_weights.1.model), custom_call_target="tpu_custom_call" | custom-call | tf_op jit(solution)/shard_map/place_weights/pallas_call | solution.py:648
  161.5 1.3 collective-permute-start
  163.5 48.4 %forward.1 = (f32[2,512,768]{2,1,0:T(8,128)}, bf16[3,1024,768]{2,1,0:T(8,128)(2,1)}, f32[2,12,512]{2,1,0:T(8,128)}, bf16[2,512,768]{2,1,0:T(8,128)(2,1)}, f32[2,...) custom-call(bf16[2,512,768]{2,1,0:T(8,128)(2,1)} %bitcast.3, ...), custom_call_target="tpu_custom_call" | custom-call | flops 16911433728 | bytes 16515072 | tf_op jit(solution)/shard_map/forward/pallas_call | solution.py:832
  211.9 17.9 %exchange_states.1 = (f32[2,512,768]{2,1,0:T(8,128)}, bf16[3,1024,768]{2,1,0:T(8,128)(2,1)}, f32[2,12,512]{2,1,0:T(8,128)}, bf16[2,512,768]{2,1,0:T(8,128)(2,1)}...) custom-call(f32[2,512,768]{2,1,0:T(8,128)} %get-tuple-element.37.ref, ...), custom_call_target="tpu_custom_call", output_to_operand_aliasing={{0}: (0, {}), {1}: (1, {}), {2}: (2, {}), {3}: (3, {}), {4}... | custom-call | tf_op jit(solution)/shard_map/exchange_states/pallas_call | solution.py:570
  229.8 0.0 collective-permute-done.w_far
  229.8 43.3 %backward.1 = (bf16[1,512,768]{2,1,0:T(8,128)(2,1)}, bf16[1,512,768]{2,1,0:T(8,128)(2,1)}, bf16[1,512,768]{2,1,0:T(8,128)(2,1)}, bf16[4,512,768]{2,1,0:T(8,128)(...) custom-call(s32[2,1,512]{2,1,0:T(1,128)} %seg.3, ...), custom_call_target="tpu_custom_call" | custom-call | tf_op jit(solution)/shard_map/backward/pallas_call | solution.py:1080
  273.1 39.9 %weight_grads.1 = bf16[32,336,768]{2,1,0:T(8,128)(2,1)} custom-call(s32[10752]{0:T(1024)} %get-tuple-element.67.places, bf16[2,512,768]{2,1,0:T(8,128)(2,1)} %bitcast.4, bf16[2,512,768]{2,1,0:T(8,128)(2,1)} %get-tuple-element.45.mixed, bf16[1,512,768]{2,1,0:T(8,128)(2,1)} %get-tuple-element.53.head, bf16[1,512,768]{2,1,0:T(8,128)(2,1)} %get-tuple-element.54.attn, ...), custom_call_target="tpu_custom_call" | custom-call | tf_op jit(solution)/shard_map/weight_grads/pallas_call | solution.py:1210
  313.0 83.9 %reduce_grads.1 = (f32[336,768]{1,0:T(8,128)}, f32[8,768]{1,0:T(8,128)}) custom-call(bf16[2,16,336,768]{3,2,1,0:T(8,128)(2,1)} %bitcast.2, f32[8,768]{1,0:T(8,128)} %get-tuple-element.63.small), custom_call_target="tpu_custom_call" | custom-call | tf_op jit(solution)/shard_map/reduce_grads/pallas_call | solution.py:457
  397.0 5.7 %update.1 = (f32[1]{0:T(128)}, f32[1]{0:T(128)}, f32[336,768]{1,0:T(8,128)}, f32[336,768]{1,0:T(8,128)}, f32[336,768]{1,0:T(8,128)}, /*index=5*/f32[336,768]{1,0:T(8,128)}, f32[4,768]{1,0:T(4,128)}, f32[4,768]{1,0:T(4,128)}) custom-call(s32[1]{0:T(128)S(6)} %copy.35.step, f32[8,768]{1,0:T(8,128)} %get-tuple-element.64.total, f32[4,768]{1,0:T(4,128)} %gains.3, ...), custom_call_target="tpu_custom_call" | custom-call | tf_op jit(solution)/shard_map/update/pallas_call | solution.py:1275
Async XLA Ops:
  161.5 68.2 %collective-permute-start = (bf16[14,768,768]{2,1,0:T(8,128)(2,1)}, bf16[14,768,768]{2,1,0:T(8,128)(2,1)}, u32[]{:S(2)}, u32[]{:S(2)}) collective-permute-start(bf16[14,768,768]{2,1,0:T(8,128)(2,1)} %place_weights.1.w_hbm.w_own), channel_id=1, source_target_pairs={{16,0},{17,1},{18,2},{19,3},{20,4},{21,5},{22,6},{23,7},{24,8},{25... | collective-permute-start | bytes 49545224 | tf_op jit(solution)/shard_map/ppermute | solution.py:1317

commit v3 on v2

--- a/solution.py
+++ b/solution.py
@@ -58,6 +58,7 @@
 
 MESH = pl.DeviceIdType.MESH
 KERNEL_CHIPS = 16
+AHEAD = 8
 
 
 def chip_grid(chips):
@@ -359,7 +360,7 @@
     def load_end(local, half):
         half.wait_send()
 
-    for where in firsts:
+    for where in firsts[:AHEAD]:
         load(where, load_start)
 
     def parent(c, r, block):
@@ -389,42 +390,26 @@
                     part, part, send_sem.at[c, block], recv_sem.at[c, slot, block], {"dp": me}, MESH
                 )
                 guarded([there], arrival.wait_recv)
-            children = [(across, None)] + children
-
+            sure = [across] + [slot for slot, there in children if there is None]
+
+            def add(slots, source, target):
+                def piece(k, carry):
+                    at = (pl.ds(pl.multiple_of(k * tall, tall), tall), slice(first, first + wide))
+                    total = source[at].astype(F32)
+                    for slot in slots:
+                        total = total + heard[(slot, block) + at].astype(F32)
+                    target[at] = total.astype(target.dtype)
+                    return carry
+
+                lax.fori_loop(0, rows // tall, piece, 0)
+
+            target = acc.at[block] if any(r) else out
+            add(sure, acc.at[block], target)
+            for slot, there in children:
+                if there is not None:
+                    pl.when(there)(functools.partial(add, [slot], target, target))
             if any(r):
-                for slot, there in children:
-
-                    def total(slot=slot):
-                        def piece(k, carry):
-                            at = (pl.ds(pl.multiple_of(k * tall, tall), tall), slice(first, first + wide))
-                            acc[(block,) + at] = (
-                                acc[(block,) + at].astype(F32) + heard[(slot, block) + at].astype(F32)
-                            ).astype(BF)
-                            return carry
-
-                        lax.fori_loop(0, rows // tall, piece, 0)
-
-                    guarded([there], total)
                 parent(c, r, block).start()
-            else:
-
-                def first_piece(k, carry):
-                    at = (pl.ds(pl.multiple_of(k * tall, tall), tall), slice(first, first + wide))
-                    out[at] = acc[(block,) + at].astype(F32)
-                    return carry
-
-                lax.fori_loop(0, rows // tall, first_piece, 0)
-                for slot, there in children:
-
-                    def total(slot=slot):
-                        def piece(k, carry):
-                            at = (pl.ds(pl.multiple_of(k * tall, tall), tall), slice(first, first + wide))
-                            out[at] = out[at] + heard[(slot, block) + at].astype(F32)
-                            return carry
-
-                        lax.fori_loop(0, rows // tall, piece, 0)
-
-                    guarded([there], total)
 
         guarded(real, run)
 
@@ -433,6 +418,8 @@
         if spot(c, r) not in ready:
             ready.add(spot(c, r))
             load(spot(c, r), load_wait)
+            for where in firsts[len(ready) + AHEAD - 1 : len(ready) + AHEAD]:
+                load(where, load_start)
         visit(c, r)
     def squares(k, carry):
         part = out[pl.ds(pl.multiple_of(k * tall, tall), tall), :]
@@ -705,15 +692,18 @@
     for j in range(cuts):
         order += [6 + j, 6 + cuts + j]
 
-    @pl.when(i == 0)
-    def _():
-        for u in order:
-            pltpu.make_async_copy(w_hbm.at[u], w.at[u], sem.at[u]).start()
+    def bring(which):
+        @pl.when(i == 0)
+        def _():
+            for u in which:
+                pltpu.make_async_copy(w_hbm.at[u], w.at[u], sem.at[u]).start()
 
     def need(u):
         @pl.when(i == 0)
         def _():
             pltpu.make_async_copy(w_hbm.at[u], w.at[u], sem.at[u]).wait()
+
+    bring(order[:2])
 
     def leave(k, b):
         tokens = pl.ds(pl.multiple_of(b * slots, slots), slots)
@@ -734,6 +724,7 @@
     fill_bias(bias, seg_col, seg_row)
     flags = flag_column(pos[0], slots) * role
     need(0)
+    bring(order[2:])
     e = nn(patch[0], w[0])
     e = jnp.where(flags > 0, gain[3:4, :], e)
     e_v[i] = e
@@ -908,6 +899,13 @@
     x2_copy = bring(0, x2_hbm.at[role], x2_in)
     bring_piece(2)
     tgt_copy = bring(1, tgt_hbm.at[role], tgt)
+    small[...] = jnp.zeros_like(small)
+
+    seg_row = seg[role]
+    seg_col = column_of(seg_row)
+    fill_bias(bias, seg_col, seg_row)
+    flags = flag_column(pos[role], slots)
+    x2_copy.wait()
     x1_copy = bring(2, x1_hbm.at[role], x1_in)
     for j in range(cuts):
         bring_piece(6 + cuts + j)
@@ -917,13 +915,6 @@
     for j in range(3):
         bring_piece(3 + j)
     e_copy = bring(4, e_hbm.at[role], e_in)
-    small[...] = jnp.zeros_like(small)
-
-    seg_row = seg[role]
-    seg_col = column_of(seg_row)
-    fill_bias(bias, seg_col, seg_row)
-    flags = flag_column(pos[role], slots)
-    x2_copy.wait()
     n3, r3 = layer_stats(x2_in[...])
     head_in = (n3 * gain[2:3, :]).astype(BF)
     head_v[...] = head_in

time: 403 us -> 400 us (level)
  transfers between devices with their start and end apart: 1 -> 1, of which waited for: 0 -> 0; matrix products, arithmetic and copies ran while one was open for 0% -> 0% of each run, Pallas kernels for 16% -> 17%
where the time goes in v3:
time: 400 us
  Pallas kernels  395 us (99%)
    pallas_call x1, Pallas kernels, gather_weights(): pl.pallas_call(functools.partial(gather_kernel, grid), name='gather_weigh...  130 us
    pallas_call x1, Pallas kernels, reduce_grads(): pl.pallas_call(functools.partial(reduce_kernel, grid), name='reduce_grads...  83.5 us
    pallas_call x1, Pallas kernels, forward(): pl.pallas_call(fwd_kernel, name='forward', grid=(batches,), out_shape=tup...  48.4 us
    pallas_call x1, Pallas kernels, backward(): pl.pallas_call(bwd_kernel, name='backward', out_shape=tuple((jax.ShapeDty...  40.3 us
    pallas_call x1, Pallas kernels, weight_grads(): pl.pallas_call(functools.partial(grads_kernel, plan), name='weight_grads'...  40 us
    pallas_call x1, Pallas kernels, place_weights(): pl.pallas_call(place_kernel, name='place_weights', out_shape=jax.ShapeDty...  29.6 us
    pallas_call x1, Pallas kernels, exchange_states(): pl.pallas_call(exchange_kernel, name='exchange_states', out_shape=tuple((...  17.9 us
  transfers between devices with their start and end apart: 1, of which 0 were waited for; matrix products, arithmetic and copies ran while one was open for 0% of the time, Pallas kernels for 17%

profile of v3, /device:TPU:0, one launch (start us, length us, event | category | flops | bytes accessed | tf_op | source)
XLA Modules:
  0.0 399.7 jit_solution(8668932839579968618)
XLA Ops:
  0.6 1.6 fusion.9
  2.2 129.7 %gather_weights.1.model = bf16[16,2,336,768]{3,2,1,0:T(8,128)(2,1)} custom-call(f32[336,768]{1,0:T(8,128)} %master.1, f32[336,768]{1,0:T(8,128)} %teacher.1), custom_call_target="tpu_custom_call" | custom-call | tf_op jit(solution)/shard_map/gather_weights/pallas_call | solution.py:259
  131.9 29.6 %place_weights.1.w_hbm.w_own = bf16[14,768,768]{2,1,0:T(8,128)(2,1)} custom-call(s32[10752]{0:T(1024)} %get-tuple-element.66.spots, bf16[16,2,336,768]{3,2,1,0:T(8,128)(2,1)} %gather_weights.1.model), custom_call_target="tpu_custom_call" | custom-call | tf_op jit(solution)/shard_map/place_weights/pallas_call | solution.py:635
  161.5 1.3 collective-permute-start
  163.5 48.4 %forward.1 = (f32[2,512,768]{2,1,0:T(8,128)}, bf16[3,1024,768]{2,1,0:T(8,128)(2,1)}, f32[2,12,512]{2,1,0:T(8,128)}, bf16[2,512,768]{2,1,0:T(8,128)(2,1)}, f32[2,...) custom-call(bf16[2,512,768]{2,1,0:T(8,128)(2,1)} %bitcast.3, ...), custom_call_target="tpu_custom_call" | custom-call | flops 16911433728 | bytes 16515072 | tf_op jit(solution)/shard_map/forward/pallas_call | solution.py:823
  211.9 17.9 %exchange_states.1 = (f32[2,512,768]{2,1,0:T(8,128)}, bf16[3,1024,768]{2,1,0:T(8,128)(2,1)}, f32[2,12,512]{2,1,0:T(8,128)}, bf16[2,512,768]{2,1,0:T(8,128)(2,1)}...) custom-call(f32[2,512,768]{2,1,0:T(8,128)} %get-tuple-element.37.ref, ...), custom_call_target="tpu_custom_call", output_to_operand_aliasing={{0}: (0, {}), {1}: (1, {}), {2}: (2, {}), {3}: (3, {}), {4}... | custom-call | tf_op jit(solution)/shard_map/exchange_states/pallas_call | solution.py:557
  229.8 0.0 collective-permute-done.w_far
  229.8 40.3 %backward.1 = (bf16[1,512,768]{2,1,0:T(8,128)(2,1)}, bf16[1,512,768]{2,1,0:T(8,128)(2,1)}, bf16[1,512,768]{2,1,0:T(8,128)(2,1)}, bf16[4,512,768]{2,1,0:T(8,128)(...) custom-call(s32[2,1,512]{2,1,0:T(1,128)} %seg.3, ...), custom_call_target="tpu_custom_call" | custom-call | tf_op jit(solution)/shard_map/backward/pallas_call | solution.py:1071
  270.1 40.0 %weight_grads.1 = bf16[32,336,768]{2,1,0:T(8,128)(2,1)} custom-call(s32[10752]{0:T(1024)} %get-tuple-element.67.places, bf16[2,512,768]{2,1,0:T(8,128)(2,1)} %bitcast.4, bf16[2,512,768]{2,1,0:T(8,128)(2,1)} %get-tuple-element.45.mixed, bf16[1,512,768]{2,1,0:T(8,128)(2,1)} %get-tuple-element.53.head, bf16[1,512,768]{2,1,0:T(8,128)(2,1)} %get-tuple-element.54.attn, ...), custom_call_target="tpu_custom_call" | custom-call | tf_op jit(solution)/shard_map/weight_grads/pallas_call | solution.py:1201
  310.1 83.5 %reduce_grads.1 = (f32[336,768]{1,0:T(8,128)}, f32[8,768]{1,0:T(8,128)}) custom-call(bf16[2,16,336,768]{3,2,1,0:T(8,128)(2,1)} %bitcast.2, f32[8,768]{1,0:T(8,128)} %get-tuple-element.63.small), custom_call_target="tpu_custom_call" | custom-call | tf_op jit(solution)/shard_map/reduce_grads/pallas_call | solution.py:444
  393.6 5.9 %update.1 = (f32[1]{0:T(128)}, f32[1]{0:T(128)}, f32[336,768]{1,0:T(8,128)}, f32[336,768]{1,0:T(8,128)}, f32[336,768]{1,0:T(8,128)}, /*index=5*/f32[336,768]{1,0:T(8,128)}, f32[4,768]{1,0:T(4,128)}, f32[4,768]{1,0:T(4,128)}) custom-call(s32[1]{0:T(128)S(6)} %copy.35.step, f32[8,768]{1,0:T(8,128)} %get-tuple-element.64.total, f32[4,768]{1,0:T(4,128)} %gains.3, ...), custom_call_target="tpu_custom_call" | custom-call | tf_op jit(solution)/shard_map/update/pallas_call | solution.py:1266
Async XLA Ops:
  161.5 68.2 %collective-permute-start = (bf16[14,768,768]{2,1,0:T(8,128)(2,1)}, bf16[14,768,768]{2,1,0:T(8,128)(2,1)}, u32[]{:S(2)}, u32[]{:S(2)}) collective-permute-start(bf16[14,768,768]{2,1,0:T(8,128)(2,1)} %place_weights.1.w_hbm.w_own), channel_id=1, source_target_pairs={{16,0},{17,1},{18,2},{19,3},{20,4},{21,5},{22,6},{23,7},{24,8},{25... | collective-permute-start | bytes 49545224 | tf_op jit(solution)/shard_map/ppermute | solution.py:1308

commit v4 on v3

--- a/solution.py
+++ b/solution.py
@@ -579,7 +579,7 @@
     blocks = cores * chips
     cols = width // LANES
     deep, wide = inbuf.shape[0], outbuf.shape[0]
-    group = max([g for g in range(1, 17) if rows % g == 0])
+    group = max([g for g in range(1, 49) if rows % g == 0])
 
     def fetch(b, slot):
         return pltpu.make_async_copy(model.at[lax.rem(b, chips), b // chips], inbuf.at[slot], in_sem.at[slot])
@@ -667,8 +667,19 @@
     return jnp.max(jnp.where(hit, 1, 0), axis=1, keepdims=True)
 
 
-def fill_bias(bias, seg_col, seg_row):
-    bias[...] = jnp.where(seg_col == seg_row, 0.0, MASK_FILL)
+def fill_masks(k_mask, q_mask, seg_col):
+    lane = lax.broadcasted_iota(jnp.int32, (1, LANES), 1)
+    for h in range(2):
+        at = lane - (HEAD_DIM if h == 0 else 0)
+        same = at == seg_col
+        other = jnp.logical_and(jnp.logical_and(at >= 0, at <= IMGS), jnp.logical_not(same))
+        k_mask[h] = jnp.where(same, 1.0, 0.0).astype(BF)
+        q_mask[h] = jnp.where(other, MASK_FILL, 0.0).astype(BF)
+
+
+def masked(x, mask, h):
+    low = lax.broadcasted_iota(jnp.int32, (1, LANES), 1) < HEAD_DIM
+    return jnp.where(low if h == 0 else jnp.logical_not(low), x, mask[h])
 
 
 def half(x, h):
@@ -680,7 +691,7 @@
 def fwd_kernel(
     patch, seg, pos, gains, teacher_gains, w_hbm,
     e_out, qkv_out, lse_out, o_out, x1_out, x2_out, tgt_out, bank_out,
-    w, bias, gain, a2, e_v, qkv, lse, o_v, x1_v, x2_v, tgt, bank, sem, out_sem,
+    w, k_mask, q_mask, gain, a2, e_v, qkv, lse, o_v, x1_v, x2_v, tgt, bank, sem, out_sem,
 ):
     i = pl.program_id(0)
     role = lax.axis_index("group")
@@ -721,7 +732,7 @@
 
     seg_row = seg[0]
     seg_col = column_of(seg_row)
-    fill_bias(bias, seg_col, seg_row)
+    fill_masks(k_mask, q_mask, seg_col)
     flags = flag_column(pos[0], slots) * role
     need(0)
     bring(order[2:])
@@ -746,7 +757,7 @@
         v_t = v2.T
         outs = []
         for h in range(2):
-            s = nt(half(k2, h), q2) + bias[...]
+            s = nt(masked(k2, k_mask, h), masked(q2, q_mask, h))
             top = jnp.max(s, axis=0, keepdims=True)
             ex = jnp.exp(s - top)
             total = jnp.sum(ex, axis=0, keepdims=True)
@@ -836,7 +847,8 @@
         out_specs=(any_spec(),) * len(outs),
         scratch_shapes=[
             pltpu.VMEM((pieces, width, width), BF),
-            pltpu.VMEM((slots, slots), F32),
+            pltpu.VMEM((2, slots, LANES), BF),
+            pltpu.VMEM((2, slots, LANES), BF),
             pltpu.VMEM((4, width), F32),
             pltpu.VMEM((slots, width), BF),
         ]
@@ -862,7 +874,7 @@
 def bwd_kernel(
     seg, pos, gain, lse, banks, e_hbm, qkv_hbm, x1_hbm, x2_hbm, tgt_hbm, w_own, w_far,
     head_out, attn_out, ffn_out, act_out, de_out, mid_out, pred_out, dqkv_out, du_out, down_out, small,
-    w, bias, top_scr, acc_scr, pool_scr, bank_scr, e_in, qkv, x1_in, x2_in, tgt,
+    w, k_mask, q_mask, top_scr, acc_scr, pool_scr, bank_scr, e_in, qkv, x1_in, x2_in, tgt,
     head_v, attn_v, ffn_v, act_v, de_v, mid_v, pred_v, dqkv, du_v, down_v, sem, in_sem, out_sem,
 ):
     role, chip = lax.axis_index("group"), lax.axis_index("dp")
@@ -903,7 +915,7 @@
 
     seg_row = seg[role]
     seg_col = column_of(seg_row)
-    fill_bias(bias, seg_col, seg_row)
+    fill_masks(k_mask, q_mask, seg_col)
     flags = flag_column(pos[role], slots)
     x2_copy.wait()
     x1_copy = bring(2, x1_hbm.at[role], x1_in)
@@ -1023,7 +1035,7 @@
         k_t = k2.T
         dq, dk, dv = [], 0.0, 0.0
         for h in range(2):
-            s = nt(half(k_scaled, h), q2) + bias[...]
+            s = nt(masked(k_scaled, k_mask, h), masked(q2, q_mask, h))
             probs = jnp.exp(s - lse[role, pl.ds(2 * p + h, 1), :])
             dp = nt(half(v2, h), g2)
             centre = jnp.sum(probs * dp, axis=0, keepdims=True)
@@ -1077,7 +1089,8 @@
         out_specs=(any_spec(),) * len(counts) + (vmem,),
         scratch_shapes=[
             pltpu.VMEM((pieces - 1, width, width), BF),
-            pltpu.VMEM((slots, slots), F32),
+            pltpu.VMEM((2, slots, LANES), BF),
+            pltpu.VMEM((2, slots, LANES), BF),
             pltpu.VMEM((slots, width), F32),
             pltpu.VMEM((slots, width), F32),
             pltpu.VMEM((SUBLANES, width), F32),
@@ -1132,18 +1145,18 @@
         else:
             fresh_r = False
         steps.append((u, len(lkeys) - 1, fresh_l, len(rkeys) - 1, fresh_r))
-    for copy in lcopies[: deep - 1] + rcopies[: deep - 1]:
-        copy.start()
+    lcopies[0].start()
+    rcopies[0].start()
     for u, li, fresh_l, ri, fresh_r in steps:
         if fresh_l:
             lcopies[li].wait()
-            if li + deep - 1 < len(lcopies):
-                lcopies[li + deep - 1].start()
+            for copy in lcopies[1:deep] if li == 0 else lcopies[li + deep - 1 : li + deep]:
+                copy.start()
             x_t[...] = x_buf[li % deep].T
         if fresh_r:
             rcopies[ri].wait()
-            if ri + deep - 1 < len(rcopies):
-                rcopies[ri + deep - 1].start()
+            for copy in rcopies[1:deep] if ri == 0 else rcopies[ri + deep - 1 : ri + deep]:
+                copy.start()
         wide = 2 * LANES
 
         def tile(n, carry):

time: 400 us -> 397 us (level)
  no operation moved by 1% of the time
where the time goes in v4:
time: 397 us
  Pallas kernels  392 us (99%)
    pallas_call x1, Pallas kernels, gather_weights(): pl.pallas_call(functools.partial(gather_kernel, grid), name='gather_weigh...  130 us
    pallas_call x1, Pallas kernels, reduce_grads(): pl.pallas_call(functools.partial(reduce_kernel, grid), name='reduce_grads...  83.5 us
    pallas_call x1, Pallas kernels, forward(): pl.pallas_call(fwd_kernel, name='forward', grid=(batches,), out_shape=tup...  48.3 us
    pallas_call x1, Pallas kernels, backward(): pl.pallas_call(bwd_kernel, name='backward', out_shape=tuple((jax.ShapeDty...  40.3 us
    pallas_call x1, Pallas kernels, weight_grads(): pl.pallas_call(functools.partial(grads_kernel, plan), name='weight_grads'...  39.8 us
    pallas_call x1, Pallas kernels, place_weights(): pl.pallas_call(place_kernel, name='place_weights', out_shape=jax.ShapeDty...  26.9 us
    pallas_call x1, Pallas kernels, exchange_states(): pl.pallas_call(exchange_kernel, name='exchange_states', out_shape=tuple((...  17.9 us
  transfers between devices with their start and end apart: 1, of which 0 were waited for; matrix products, arithmetic and copies ran while one was open for 0% of the time, Pallas kernels for 17%

profile of v4, /device:TPU:0, one launch (start us, length us, event | category | flops | bytes accessed | tf_op | source)
XLA Modules:
  0.0 396.7 jit_solution(4148680220779012938)
XLA Ops:
  0.6 1.6 fusion.9
  2.2 129.7 %gather_weights.1.model = bf16[16,2,336,768]{3,2,1,0:T(8,128)(2,1)} custom-call(f32[336,768]{1,0:T(8,128)} %master.1, f32[336,768]{1,0:T(8,128)} %teacher.1), custom_call_target="tpu_custom_call" | custom-call | tf_op jit(solution)/shard_map/gather_weights/pallas_call | solution.py:259
  131.9 26.9 %place_weights.1.w_hbm.w_own = bf16[14,768,768]{2,1,0:T(8,128)(2,1)} custom-call(s32[10752]{0:T(1024)} %get-tuple-element.66.spots, bf16[16,2,336,768]{3,2,1,0:T(8,128)(2,1)} %gather_weights.1.model), custom_call_target="tpu_custom_call" | custom-call | tf_op jit(solution)/shard_map/place_weights/pallas_call | solution.py:635
  158.8 1.3 collective-permute-start
  160.7 48.3 %forward.1 = (f32[2,512,768]{2,1,0:T(8,128)}, bf16[3,1024,768]{2,1,0:T(8,128)(2,1)}, f32[2,12,512]{2,1,0:T(8,128)}, bf16[2,512,768]{2,1,0:T(8,128)(2,1)}, f32[2,...) custom-call(bf16[2,512,768]{2,1,0:T(8,128)(2,1)} %bitcast.3, ...), custom_call_target="tpu_custom_call" | custom-call | flops 16911433728 | bytes 16515072 | tf_op jit(solution)/shard_map/forward/pallas_call | solution.py:834
  209.1 17.9 %exchange_states.1 = (f32[2,512,768]{2,1,0:T(8,128)}, bf16[3,1024,768]{2,1,0:T(8,128)(2,1)}, f32[2,12,512]{2,1,0:T(8,128)}, bf16[2,512,768]{2,1,0:T(8,128)(2,1)}...) custom-call(f32[2,512,768]{2,1,0:T(8,128)} %get-tuple-element.37.ref, ...), custom_call_target="tpu_custom_call", output_to_operand_aliasing={{0}: (0, {}), {1}: (1, {}), {2}: (2, {}), {3}: (3, {}), {4}... | custom-call | tf_op jit(solution)/shard_map/exchange_states/pallas_call | solution.py:557
  226.9 0.0 collective-permute-done.w_far
  226.9 40.3 %backward.1 = (bf16[1,512,768]{2,1,0:T(8,128)(2,1)}, bf16[1,512,768]{2,1,0:T(8,128)(2,1)}, bf16[1,512,768]{2,1,0:T(8,128)(2,1)}, bf16[4,512,768]{2,1,0:T(8,128)(...) custom-call(s32[2,1,512]{2,1,0:T(1,128)} %seg.3, ...), custom_call_target="tpu_custom_call" | custom-call | tf_op jit(solution)/shard_map/backward/pallas_call | solution.py:1083
  267.3 39.8 %weight_grads.1 = bf16[32,336,768]{2,1,0:T(8,128)(2,1)} custom-call(s32[10752]{0:T(1024)} %get-tuple-element.67.places, bf16[2,512,768]{2,1,0:T(8,128)(2,1)} %bitcast.4, bf16[2,512,768]{2,1,0:T(8,128)(2,1)} %get-tuple-element.45.mixed, bf16[1,512,768]{2,1,0:T(8,128)(2,1)} %get-tuple-element.53.head, bf16[1,512,768]{2,1,0:T(8,128)(2,1)} %get-tuple-element.54.attn, ...), custom_call_target="tpu_custom_call" | custom-call | tf_op jit(solution)/shard_map/weight_grads/pallas_call | solution.py:1214
  307.0 83.5 %reduce_grads.1 = (f32[336,768]{1,0:T(8,128)}, f32[8,768]{1,0:T(8,128)}) custom-call(bf16[2,16,336,768]{3,2,1,0:T(8,128)(2,1)} %bitcast.2, f32[8,768]{1,0:T(8,128)} %get-tuple-element.63.small), custom_call_target="tpu_custom_call" | custom-call | tf_op jit(solution)/shard_map/reduce_grads/pallas_call | solution.py:444
  390.5 6.0 %update.1 = (f32[1]{0:T(128)}, f32[1]{0:T(128)}, f32[336,768]{1,0:T(8,128)}, f32[336,768]{1,0:T(8,128)}, f32[336,768]{1,0:T(8,128)}, /*index=5*/f32[336,768]{1,0:T(8,128)}, f32[4,768]{1,0:T(4,128)}, f32[4,768]{1,0:T(4,128)}) custom-call(s32[1]{0:T(128)S(6)} %copy.35.step, f32[8,768]{1,0:T(8,128)} %get-tuple-element.64.total, f32[4,768]{1,0:T(4,128)} %gains.3, ...), custom_call_target="tpu_custom_call" | custom-call | tf_op jit(solution)/shard_map/update/pallas_call | solution.py:1279
Async XLA Ops:
  158.8 68.2 %collective-permute-start = (bf16[14,768,768]{2,1,0:T(8,128)(2,1)}, bf16[14,768,768]{2,1,0:T(8,128)(2,1)}, u32[]{:S(2)}, u32[]{:S(2)}) collective-permute-start(bf16[14,768,768]{2,1,0:T(8,128)(2,1)} %place_weights.1.w_hbm.w_own), channel_id=1, source_target_pairs={{16,0},{17,1},{18,2},{19,3},{20,4},{21,5},{22,6},{23,7},{24,8},{25... | collective-permute-start | bytes 49545224 | tf_op jit(solution)/shard_map/ppermute | solution.py:1321
